TPU v7x, 32 devices: a whole 2x2x4 slice. The times are simulated.
32 devices in a mesh: row: 16 (over z, y, x), col: 2 (over core).
Axes of the slice: x: 2, y: 2, z: 4, core: 2. Of those that a mesh axis runs over, the one named last changes fastest.
Arguments:
- image_embeddings: bfloat16 [128, 64, 1024], P('row', 'col'), may hold values from -6 to 6
- lagged_blend_ratios: float32 [3, 1024], replicated, may hold values from 0.05 to 0.95
- linear_map_coefficients: bfloat16 [3, 1024, 1024], P(None, 'row'), may hold values from -0.1875 to 0.1875
- retention_exponent: float32 [16, 128, 64], P(None, 'row', 'col'), may hold values from -3 to 0, as said below
- self_credit: float32 [1024], replicated, may hold values from 1 to 8
- channel_scale_vector: float32 [1024], replicated, may hold values from 0.5 to 2
- pooling_scale_vector: float32 [4096], replicated, may hold values from 0.5 to 2
- pooling_offset_vector: float32 [4096], replicated, may hold values from -3 to 3
Outputs:
- merged: bfloat16 [64, 32, 4096], P('row', 'col')
Inputs may be any that keep to these rules, and one draw needn't show every extreme that they name: `retention_exponent`: the logarithm of the share of a head's state kept at each patch.
All inputs are finite; a program needn't handle non-finite values.
Results may differ from a plain program's by a relative error of at most 0.0057.
Values may be sent and summed in bfloat16 or wider, within the bound.
A program may use at most 192 MiB of HBM per device.

v0:
```python
import functools

import jax
import jax.numpy as jnp
from jax import lax
from jax.experimental import pallas as pl
from jax.experimental.pallas import tpu as pltpu
from jax.sharding import PartitionSpec as P

MESH = pl.DeviceIdType.MESH
F32 = jnp.float32
BF16 = jnp.bfloat16
HIGH = lax.Precision.HIGHEST
UP, DOWN, FIRST, SECOND, MATE = range(5)


def iota(shape, dim):
    return lax.broadcasted_iota(jnp.int32, shape, dim)


def kernel(
    rows, cols, tile_rows, tile_cols, heads,
    x_ref, ratio_ref, w_ref, ret_ref, credit_ref, gain_ref, scale_ref, offset_ref,
    out_ref,
    wf, mx, proj, decay, halo_side, halo_row, run_c, mine, totals, kept_all, states, arrived, scan_f, leaving,
    entering, block, stats,
    w_send, w_recv, halo_send, halo_recv, t_send, t_recv, a_send, a_recv, b_send, b_recv,
):
    count, width = x_ref.shape
    hd = width // heads
    pairs = heads // 2
    lanes = 2 * hd
    quarter = width // 4
    share = w_ref.shape[1]
    half_w = width // 2
    unit = states.shape[1]
    row, col = lax.axis_index("row"), lax.axis_index("col")
    plane = 4
    depth = rows // plane
    z, q = row // plane, row % plane
    bx, by = q % 2, q // 2
    half = col % 2
    mate = col + 1 - 2 * half
    q1 = (1 - half) * (q + 1 - 2 * bx) + half * (q + 2 - 4 * by)
    q2 = half * (q + 1 - 2 * bx) + (1 - half) * (q + 2 - 4 * by)
    q12 = plane - 1 - q

    barrier = pltpu.get_barrier_semaphore()
    right, left = (col + 1) % cols, (col + cols - 1) % cols
    down_row, up_row = (row + 1) % rows, (row + rows - 1) % rows
    can_up, can_down = z < depth - 1, z > 0
    has_next, has_previous = row < rows - 1, row > 0

    def greet(target):
        pl.semaphore_signal(barrier, inc=1, device_id=target, device_id_type=MESH)

    greet({"row": z * plane + q1})
    greet({"row": z * plane + q2})
    for other in (right, left, mate):
        greet({"col": other})
    for there, target in (
        (can_up, (row + plane) % rows), (can_down, (row + rows - plane) % rows),
        (has_next, down_row), (has_previous, up_row),
    ):
        @pl.when(there)
        def _():
            greet({"row": target})

    expected = (
        5 + can_up.astype(jnp.int32) + can_down.astype(jnp.int32)
        + has_next.astype(jnp.int32) + has_previous.astype(jnp.int32)
    )
    pl.semaphore_wait(barrier, expected)

    halos = [
        pltpu.make_async_remote_copy(
            x_ref.at[:, 0:quarter], halo_side.at[0], halo_send.at[0], halo_recv.at[0],
            device_id={"col": right}, device_id_type=MESH),
        pltpu.make_async_remote_copy(
            x_ref.at[:, quarter:2 * quarter], halo_side.at[1], halo_send.at[1], halo_recv.at[1],
            device_id={"col": left}, device_id_type=MESH),
        pltpu.make_async_remote_copy(
            x_ref.at[count - tile_cols:count, 2 * quarter:3 * quarter], halo_row.at[0],
            halo_send.at[2], halo_recv.at[2], device_id={"row": down_row}, device_id_type=MESH),
        pltpu.make_async_remote_copy(
            x_ref.at[0:tile_cols, 3 * quarter:], halo_row.at[1],
            halo_send.at[3], halo_recv.at[3], device_id={"row": up_row}, device_id_type=MESH),
    ]

    def sl(g):
        return (g + 1) % 3

    def place(g, side, src):
        return wf.at[sl(g), side, pl.ds(pl.multiple_of(src * share, share), share), :]

    targets = {
        UP: {"row": (row + plane) % rows},
        DOWN: {"row": (row + rows - plane) % rows},
        FIRST: {"row": z * plane + q1},
        SECOND: {"row": z * plane + q2},
        MATE: {"col": mate},
    }

    def send(g, kind, src, own=False):
        source = place(g, half, src)
        if own:
            source = w_ref.at[sl(g), :, pl.ds(pl.multiple_of(half * half_w, half_w), half_w)]
        return pltpu.make_async_remote_copy(
            source, place(g, half, src), w_send.at[g, kind, src], w_recv.at[g, half, src],
            device_id=targets[kind], device_id_type=MESH)

    def got(g, side, src):
        ref = place(g, side, src)
        pltpu.make_async_remote_copy(
            ref, ref, w_send.at[g, MATE, src], w_recv.at[g, side, src],
            device_id=targets[MATE], device_id_type=MESH).wait_recv()

    def own_step(g):
        @pl.when(can_up)
        def _():
            send(g, UP, row, True).start()

        @pl.when(can_down)
        def _():
            send(g, DOWN, row, True).start()

        send(g, SECOND, row, True).start()
        send(g, FIRST, row, True).start()

    def both(d, act):
        if d == 0:
            act(z, None)
            return

        @pl.when(z >= d)
        def _():
            act(z - d, UP)

        @pl.when(z + d < depth)
        def _():
            act(z + d, DOWN)

    def z_step(g, d):
        def act(zz, onward):
            src = zz * plane + q
            got(g, half, src)

            @pl.when(can_up if onward == UP else can_down)
            def _():
                send(g, onward, src).start()

            for kind in (SECOND, FIRST, MATE):
                send(g, kind, src).start()

        both(d, act)

    def first_step(g, d):
        def act(zz, onward):
            src = zz * plane + q1
            got(g, half, src)
            send(g, SECOND, src).start()
            send(g, MATE, src).start()

        both(d, act)

    def second_step(g, d):
        def act(zz, onward):
            for qq in (q2, q12):
                src = zz * plane + qq
                got(g, half, src)
                send(g, MATE, src).start()

        both(d, act)

    def mate_wait(g):
        def one(o, carry):
            got(g, 1 - half, (row + o) % rows)
            return carry

        lax.fori_loop(1, rows, one, 0)

    own_step(0)
    own_step(1)
    halos[0].start()
    halos[1].start()

    @pl.when(has_next)
    def _():
        halos[2].start()

    @pl.when(has_previous)
    def _():
        halos[3].start()

    own_step(2)

    at = pl.ds(pl.multiple_of(row * share, share), share)
    for p in range(3):
        for side in range(2):
            wf[p, side, at, :] = w_ref[p, :, side * half_w:(side + 1) * half_w]

    ret = jnp.concatenate([ret_ref[:, r, :] for r in range(tile_rows)], axis=1)
    tri = (iota((count, count), 0) >= iota((count, count), 1)).astype(F32)
    running_c = lax.dot_general(tri, ret, (((1,), (1,)), ((), ())), precision=HIGH, preferred_element_type=F32)
    running_r = lax.dot_general(ret, tri, (((1,), (1,)), ((), ())), precision=HIGH, preferred_element_type=F32)
    eye = (iota((count, count), 0) == iota((count, count), 1)).astype(F32)
    ret_c = lax.dot_general(eye, ret, (((1,), (1,)), ((), ())), precision=HIGH, preferred_element_type=F32)
    before_c = running_c - ret_c
    before_r = running_r - ret
    total_r = running_c[count - 1:count, :]
    run_c[0] = running_c
    run_c[1] = before_c
    run_c[2] = total_r - running_c
    mine[...] = jnp.broadcast_to(
        jnp.concatenate([total_r, jnp.zeros((1, 128 - heads), F32)], axis=1), (8, 128))
    totals[row] = mine[...]

    def picked(table, h):
        return jnp.sum(jnp.where(iota(table.shape, 1) == h, table, 0.0), axis=1, keepdims=True)

    def picked_row(table, h):
        return jnp.sum(jnp.where(iota(table.shape, 0) == h, table, 0.0), axis=0, keepdims=True)

    def total_copy(o):
        to = (row + o) % rows
        return pltpu.make_async_remote_copy(
            mine, totals.at[row], t_send.at[to], t_recv.at[row],
            device_id={"row": to}, device_id_type=MESH)

    def total_send(o, carry):
        total_copy(o).start()
        return carry

    issued = set()

    def once(step, g, d):
        if d < depth and (step, g, d) not in issued:
            issued.add((step, g, d))
            step(g, d)

    def z_steps(groups, d):
        for g in groups:
            once(z_step, g, d)

    def first_steps(groups, d):
        for g in groups:
            once(first_step, g, d)

    def second_steps(groups, d):
        for g in groups:
            once(second_step, g, d)

    early = (0, 1)
    z_steps(early, 1)
    first_steps(early, 0)
    z_steps(early, 2)
    first_steps(early, 1)

    halos[0].wait()
    halos[1].wait()

    @pl.when(has_next)
    def _():
        halos[2].wait_send()
        halos[3].wait_recv()

    @pl.when(has_previous)
    def _():
        halos[3].wait_send()
        halos[2].wait_recv()

    token = iota((count, quarter), 0)
    place_in_row = token % tile_cols
    x0 = x_ref[:, 0:quarter].astype(F32)
    x1 = x_ref[:, quarter:2 * quarter].astype(F32)
    side0 = jnp.where(col > 0, halo_side[0].astype(F32), 0.0)
    side1 = jnp.where(col < cols - 1, halo_side[1].astype(F32), 0.0)
    top = jnp.where(row > 0, halo_row[0].astype(F32), 0.0)
    bottom = jnp.where(row < rows - 1, halo_row[1].astype(F32), 0.0)
    last = tile_cols - 1
    shifted = [
        jnp.where(place_in_row == 0, pltpu.roll(side0, count - last, 0), pltpu.roll(x0, 1, 0)),
        jnp.where(place_in_row == last, pltpu.roll(side1, last, 0), pltpu.roll(x1, count - 1, 0)),
        jnp.concatenate([top, x_ref[0:count - tile_cols, 2 * quarter:3 * quarter].astype(F32)], axis=0),
        jnp.concatenate([x_ref[tile_cols:count, 3 * quarter:].astype(F32), bottom], axis=0),
    ]
    for part in range(4):
        span = slice(part * quarter, (part + 1) * quarter)
        xs = x_ref[:, span].astype(F32)
        for p in range(3):
            c = ratio_ref[p:p + 1, span]
            mx[p, :, span] = (xs * c + shifted[part] * (1.0 - c)).astype(BF16)

    earlier = iota((count, count), 0) > iota((count, count), 1)
    diagonal = iota((count, count), 0) == iota((count, count), 1)

    def decays(h, carry):
        rc, bc = picked(run_c[0], h), picked(run_c[1], h)
        rr, br = picked_row(running_r, h), picked_row(before_r, h)
        exponent = jnp.where(earlier, bc - rr, br - rc)
        decay[h] = jnp.where(diagonal, 0.0, jnp.exp(exponent))
        return carry

    for d in range(3, depth):
        z_steps(early, d)
        first_steps(early, d - 1)
    z_steps((2,), 1)
    first_steps((2,), 0)
    first_steps(early, depth - 1)
    lax.fori_loop(0, heads // 2, decays, 0)
    z_steps((2,), 2)
    first_steps((2,), 1)
    for d in range(depth - 1):
        second_steps(early, d)
    lax.fori_loop(heads // 2, heads, decays, 0)
    for d in range(3, depth):
        z_steps((2,), d)
        first_steps((2,), d - 1)
    first_steps((2,), depth - 1)
    second_steps(early, depth - 1)

    def project(p):
        for side in range(2):
            def chunk(i, carry):
                src = pl.ds(pl.multiple_of(i * 256, 256), 256)
                dst = pl.ds(pl.multiple_of(side * half_w + i * 256, 256), 256)
                proj[p, :, dst] = jnp.dot(
                    mx[p], wf[p, side, :, src], preferred_element_type=F32).astype(BF16)
                return carry

            lax.fori_loop(0, half_w // 256, chunk, 0)

    mate_wait(0)
    project(1)
    mate_wait(1)
    project(2)

    lane = iota((count, lanes), 1)
    low = lane < hd

    def pair_col(table, i):
        return jnp.where(low, picked(table, 2 * i), picked(table, 2 * i + 1))

    low_u = iota((hd, lanes), 1) < hd
    flat = rows * unit

    def local_states(i, carry):
        span = pl.ds(pl.multiple_of(i * lanes, lanes), lanes)
        k = proj[1, :, span].astype(F32)
        v = proj[2, :, span]
        kd = jnp.concatenate(
            [k * jnp.exp(pair_col(run_c[2], i)), k * jnp.exp(pair_col(run_c[1], i))], axis=1).astype(BF16)
        m = lax.dot_general(kd, v, (((0,), (0,)), ((), ())), preferred_element_type=F32)
        a = jnp.where(low_u, m[0:hd], pltpu.roll(m[2 * hd:3 * hd], hd, 1)).astype(BF16)
        b = jnp.where(low_u, pltpu.roll(m[hd:2 * hd], hd, 1), m[3 * hd:]).astype(BF16)
        per = hd // unit
        for s in range(per):
            states[2 * i * per + s] = a[s * unit:(s + 1) * unit]
            states[(2 * i + 1) * per + s] = b[s * unit:(s + 1) * unit]
        return carry

    lax.fori_loop(0, pairs, local_states, 0)

    def a_copy(o):
        to = (row + o) % rows
        return pltpu.make_async_remote_copy(
            states.at[to], arrived.at[row], a_send.at[to], a_recv.at[row],
            device_id={"row": to}, device_id_type=MESH)

    def a_start(o, carry):
        a_copy(o).start()
        return carry

    lax.fori_loop(1, rows, total_send, 0)
    lax.fori_loop(1, rows, a_start, 0)
    arrived[row] = states[row]

    for d in range(depth - 1):
        second_steps((2,), d)

    def from_all(dst, send_sem, recv_sem):
        def one(o, carry):
            src = (row + o) % rows
            pltpu.make_async_remote_copy(
                dst.at[src], dst.at[src], send_sem.at[src], recv_sem.at[src],
                device_id={"row": src}, device_id_type=MESH).wait_recv()
            return carry

        lax.fori_loop(1, rows, one, 0)

    from_all(totals, t_send, t_recv)
    from_all(arrived, a_send, a_recv)
    head = (row * unit) // hd

    everyone = totals[...]
    here = iota(everyone.shape, 2) == head
    kept_all[...] = jnp.broadcast_to(
        jnp.exp(jnp.sum(jnp.where(here, everyone, 0.0), axis=2, keepdims=True)), everyone.shape)

    def kept(j):
        return kept_all[j][0:1, :]

    def forward(j, acc):
        scan_f[j] = acc
        return kept(j) * acc + arrived[j].astype(F32)

    def backward(o, acc):
        j = rows - 1 - o
        leaving[j] = jnp.where(iota((unit, lanes), 1) < hd, scan_f[j], acc).astype(BF16)
        return kept(j) * acc + arrived[j].astype(F32)

    lax.fori_loop(0, rows, forward, jnp.zeros((unit, lanes), F32))
    lax.fori_loop(0, rows, backward, jnp.zeros((unit, lanes), F32))

    def b_copy(o):
        to = (row + o) % rows
        return pltpu.make_async_remote_copy(
            leaving.at[to], entering.at[row], b_send.at[to], b_recv.at[row],
            device_id={"row": to}, device_id_type=MESH)

    def b_start(o, carry):
        b_copy(o).start()
        return carry

    lax.fori_loop(1, rows, b_start, 0)
    entering[row] = leaving[row]

    second_steps((2,), depth - 1)
    mate_wait(2)
    project(0)

    def halves(value):
        a = jnp.sum(jnp.where(low, value, 0.0), axis=1, keepdims=True)
        b = jnp.sum(jnp.where(low, 0.0, value), axis=1, keepdims=True)
        return jnp.where(low, a, b)

    def local_mix(i, carry):
        span = pl.ds(pl.multiple_of(i * lanes, lanes), lanes)
        r, k, v = proj[0, :, span], proj[1, :, span], proj[2, :, span]
        outs = []
        for s in range(2):
            rs = jnp.where(low if s == 0 else jnp.logical_not(low), r.astype(F32), 0.0).astype(BF16)
            scores = lax.dot_general(rs, k, (((1,), (1,)), ((), ())), preferred_element_type=F32)
            weight = (scores * decay[2 * i + s]).astype(BF16)
            outs.append(jnp.dot(weight, v, preferred_element_type=F32))
        own = halves(r.astype(F32) * credit_ref[:, span] * k.astype(F32)) * v.astype(F32)
        block[i] = jnp.where(low, outs[0], outs[1]) + own
        return carry

    lax.fori_loop(0, pairs, local_mix, 0)
    from_all(entering, b_send, b_recv)

    def finish(i, total):
        span = pl.ds(pl.multiple_of(i * lanes, lanes), lanes)
        r = proj[0, :, span]
        per = hd // unit
        a = jnp.concatenate([entering[2 * i * per + s].astype(F32) for s in range(per)], axis=0)
        b = jnp.concatenate([entering[(2 * i + 1) * per + s].astype(F32) for s in range(per)], axis=0)
        fwd = jnp.concatenate(
            [jnp.where(low_u, a, 0.0), jnp.where(low_u, 0.0, pltpu.roll(b, hd, 1))], axis=0).astype(BF16)
        bwd = jnp.concatenate(
            [jnp.where(low_u, pltpu.roll(a, hd, 1), 0.0), jnp.where(low_u, 0.0, b)], axis=0).astype(BF16)
        wkv = (
            block[i]
            + jnp.exp(pair_col(run_c[1], i)) * jnp.dot(r, fwd, preferred_element_type=F32)
            + jnp.exp(pair_col(run_c[2], i)) * jnp.dot(r, bwd, preferred_element_type=F32)
        )
        centred = wkv - halves(wkv) * (1.0 / hd)
        variance = halves(centred * centred) * (1.0 / hd)
        made = x_ref[:, span].astype(F32) + centred * lax.rsqrt(variance + 1e-05) * gain_ref[:, span]
        block[i] = made
        return total + made

    total = lax.fori_loop(0, pairs, finish, jnp.zeros((count, lanes), F32))
    group = (
        (iota((count, count), 0) // (2 * tile_cols) == iota((count, count), 1) // (2 * tile_cols))
        & (iota((count, count), 0) % tile_cols // 2 == iota((count, count), 1) % tile_cols // 2)
    ).astype(F32)

    def over_group(value):
        rowsum = jnp.broadcast_to(jnp.sum(value, axis=1, keepdims=True), (count, lanes))
        return jnp.dot(group, rowsum, precision=HIGH, preferred_element_type=F32) * (1.0 / (4 * width))

    mean = over_group(total)

    def spread(i, acc):
        dev = block[i] - mean
        return acc + dev * dev

    variance = over_group(lax.fori_loop(0, pairs, spread, jnp.zeros((count, lanes), F32)))
    stats[0] = mean
    stats[1] = lax.rsqrt(variance + 1e-05)
    half_cols = tile_cols // 2

    def emit(i, carry):
        for part in range(4):
            span = pl.ds(pl.multiple_of(part * width + i * lanes, lanes), lanes)
            g, o = scale_ref[:, span], offset_ref[:, span]
            for a in range(tile_rows // 2):
                take = pl.ds((2 * a + part % 2) * tile_cols + part // 2, half_cols, stride=2)
                value = (block[i, take, :] - stats[0, take, :]) * stats[1, take, :]
                out_ref[a, :, span] = (value * g + o).astype(BF16)
        return carry

    lax.fori_loop(0, pairs, emit, 0)

    def drain(o, carry):
        total_copy(o).wait_send()
        a_copy(o).wait_send()
        b_copy(o).wait_send()
        return carry

    lax.fori_loop(1, rows, drain, 0)
    for g in range(3):
        def z_drain(zz, carry):
            src = zz * plane + q

            @pl.when((zz <= z) & can_up)
            def _():
                send(g, UP, src).wait_send()

            @pl.when((zz >= z) & can_down)
            def _():
                send(g, DOWN, src).wait_send()

            send(g, FIRST, src).wait_send()
            send(g, SECOND, src).wait_send()
            send(g, SECOND, zz * plane + q1).wait_send()
            return carry

        lax.fori_loop(0, depth, z_drain, 0)

        def m_drain(o, carry):
            send(g, MATE, (row + o) % rows).wait_send()
            return carry

        lax.fori_loop(1, rows, m_drain, 0)


def body(x, ratios, w, retention, credit, gain, scale, offset):
    tile_rows, tile_cols, width = x.shape
    heads = retention.shape[0]
    count = tile_rows * tile_cols
    hd = width // heads
    rows, cols = lax.axis_size("row"), lax.axis_size("col")
    unit = heads * hd // rows
    pairs = heads // 2
    lanes = 2 * hd
    dma = pltpu.SemaphoreType.DMA
    return pl.pallas_call(
        functools.partial(kernel, rows, cols, tile_rows, tile_cols, heads),
        out_shape=jax.ShapeDtypeStruct((tile_rows // 2, tile_cols // 2, 4 * width), BF16),
        in_specs=[pl.BlockSpec(memory_space=pltpu.VMEM)] * 8,
        out_specs=pl.BlockSpec(memory_space=pltpu.VMEM),
        scratch_shapes=[
            pltpu.VMEM((3, 2, width, width // 2), BF16),
            pltpu.VMEM((3, count, width), BF16),
            pltpu.VMEM((3, count, width), BF16),
            pltpu.VMEM((heads, count, count), F32),
            pltpu.VMEM((2, count, width // 4), BF16),
            pltpu.VMEM((2, tile_cols, width // 4), BF16),
            pltpu.VMEM((3, count, heads), F32),
            pltpu.VMEM((8, 128), F32),
            pltpu.VMEM((rows, 8, 128), F32),
            pltpu.VMEM((rows, 8, 128), F32),
            pltpu.VMEM((rows, unit, lanes), BF16),
            pltpu.VMEM((rows, unit, lanes), BF16),
            pltpu.VMEM((rows, unit, lanes), F32),
            pltpu.VMEM((rows, unit, lanes), BF16),
            pltpu.VMEM((rows, unit, lanes), BF16),
            pltpu.VMEM((pairs, count, lanes), F32),
            pltpu.VMEM((2, count, lanes), F32),
            dma((3, 5, rows)),
            dma((3, 2, rows)),
            dma((4,)),
            dma((4,)),
            dma((rows,)),
            dma((rows,)),
            dma((rows,)),
            dma((rows,)),
            dma((rows,)),
            dma((rows,)),
        ],
        compiler_params=pltpu.CompilerParams(
            collective_id=0, has_side_effects=True, vmem_limit_bytes=60 * 1024 * 1024),
    )(
        x.reshape(count, width), ratios, w, retention,
        credit.reshape(1, width), gain.reshape(1, width),
        scale.reshape(1, 4 * width), offset.reshape(1, 4 * width),
    )


def solution(mesh):
    return jax.shard_map(
        body,
        mesh=mesh,
        in_specs=(
            P("row", "col", None),
            P(),
            P(None, "row", None),
            P(None, "row", "col"),
            P(),
            P(),
            P(),
            P(),
        ),
        out_specs=P("row", "col", None),
        check_vma=False,
    )
```

profile of v0, /device:TPU:0, one launch (start us, length us, event | category | flops | bytes accessed | tf_op | source)
XLA Modules:
  0.0 66.9 jit_solution(10516044917617979797)
XLA Ops:
  0.0 65.0 %shard_map.82 = bf16[4,16,4096]{2,1,0:T(8,128)(2,1)} custom-call(bf16[256,1024]{1,0:T(8,128)(2,1)} %bitcast.5, f32[3,1024]{1,0:T(4,128)} %ratio_ref.1, bf16[3,64,1024]{2,1,0:T(8,128)(2,1)} %w_ref.1, f32[16,8,32]{2,1,0:T(8,128)} %ret_ref.1, f32[1,1024]{1,0:T(1,128)} %bitcast.8, f32[1,1024]{1,0:T(1,128)} %bitcast.9, f32[1,4096]{1,0:T(1,128)} %bitcast.6, ...), custom_call_target="tpu_custom_call" | custom-call | tf_op jit(solution)/shard_map/pallas_call | solution.py:550
  65.0 1.9 %copy.10 = bf16[4,16,4096]{2,1,0:T(8,128)(2,1)} copy(bf16[4,16,4096]{2,1,0:T(8,128)(2,1)} %shard_map.82) | data formatting | bytes 1048576
where the time goes:
time: 67.1 us; the launch traced here: 66.9 us
  Pallas kernels  65 us (97%)
  local copies, waits for them, and re-layouts  1.87 us (3%)
    pallas_call x1, Pallas kernels, body(): pl.pallas_call(functools.partial(kernel, rows, cols, tile_rows, tile_cols...  65 us
    unnamed x1, local copies, waits for them, and re-layouts  1.87 us

commit v1 on v0

v1 whole, which is shorter than its diff:
```python
import functools

import jax
import jax.numpy as jnp
from jax import lax
from jax.experimental import pallas as pl
from jax.experimental.pallas import tpu as pltpu
from jax.sharding import PartitionSpec as P

MESH = pl.DeviceIdType.MESH
F32 = jnp.float32
BF16 = jnp.bfloat16
HIGH = lax.Precision.HIGHEST
PLANE = 4
SPLIT = 2
CHUNKS = ((1, 0), (2, 0), (1, 1), (2, 1), (0, 0), (0, 1))


def iota(shape, dim):
    return lax.broadcasted_iota(jnp.int32, shape, dim)


def two_terms(value):
    first = value.astype(BF16)
    return first, (value - first.astype(F32)).astype(BF16)


def kernel(
    rows, cols, tile_rows, tile_cols, heads,
    x_ref, ratio_ref, w_ref, ret_ref, credit_ref, gain_ref, scale_ref, offset_ref,
    out_ref,
    xv, wf, mx, proj, decay, halo_side, halo_row, rows_t, spread_t, mine, totals, kept_all, states, arrived,
    scan_f, scan_b, leaving, entering, block, stats,
    x_sem, own_sem, w_send, m_send, z_recv, f_recv, s_recv, m_recv, halo_send, halo_recv,
    t_send, t_recv, a_send, a_recv, b_send, b_recv,
):
    count, width = xv.shape
    hd = width // heads
    pairs = heads // 2
    lanes = 2 * hd
    quarter = width // 4
    share = w_ref.shape[1]
    half_w = width // 2
    cw = half_w // SPLIT
    unit = states.shape[2]
    per = hd // unit
    group_pairs = pairs // SPLIT
    side_pairs = group_pairs // 2
    row, col = lax.axis_index("row"), lax.axis_index("col")
    depth = rows // PLANE
    z, q = row // PLANE, row % PLANE
    bx, by = q % 2, q // 2
    half = col % 2
    mate = col + 1 - 2 * half
    q1 = (1 - half) * (q + 1 - 2 * bx) + half * (q + 2 - 4 * by)
    q2 = half * (q + 1 - 2 * bx) + (1 - half) * (q + 2 - 4 * by)
    q12 = PLANE - 1 - q
    first_row, second_row = z * PLANE + q1, z * PLANE + q2
    right, left = (col + 1) % cols, (col + cols - 1) % cols
    down_row, up_row = (row + 1) % rows, (row + rows - 1) % rows
    has_next, has_previous = row < rows - 1, row > 0

    barrier = pltpu.get_barrier_semaphore()

    def greet(target):
        pl.semaphore_signal(barrier, inc=1, device_id=target, device_id_type=MESH)

    for o in range(1, depth):
        greet({"row": (z + o) % depth * PLANE + q})
    greet({"row": first_row})
    greet({"row": second_row})
    for other in (right, left, mate):
        greet({"col": other})
    for there, target in ((has_next, down_row), (has_previous, up_row)):
        @pl.when(there)
        def _():
            greet({"row": target})

    x_copy = pltpu.make_async_copy(x_ref, xv, x_sem)
    x_copy.start()

    ret = jnp.concatenate([ret_ref[:, r, :] for r in range(tile_rows)], axis=1)
    tri = (iota((count, count), 0) >= iota((count, count), 1)).astype(F32)
    contract_last = (((1,), (1,)), ((), ()))
    running_c = lax.dot_general(tri, ret, contract_last, precision=HIGH, preferred_element_type=F32)
    running_r = lax.dot_general(ret, tri, contract_last, precision=HIGH, preferred_element_type=F32)
    eye = (iota((count, count), 0) == iota((count, count), 1)).astype(F32)
    ret_c = lax.dot_general(eye, ret, contract_last, precision=HIGH, preferred_element_type=F32)

    pl.semaphore_wait(
        barrier, depth - 1 + 5 + has_next.astype(jnp.int32) + has_previous.astype(jnp.int32))

    halos = [
        pltpu.make_async_remote_copy(
            x_ref.at[:, 0:quarter], halo_side.at[0], halo_send.at[0], halo_recv.at[0],
            device_id={"col": right}, device_id_type=MESH),
        pltpu.make_async_remote_copy(
            x_ref.at[:, quarter:2 * quarter], halo_side.at[1], halo_send.at[1], halo_recv.at[1],
            device_id={"col": left}, device_id_type=MESH),
        pltpu.make_async_remote_copy(
            x_ref.at[count - tile_cols:count, 2 * quarter:3 * quarter], halo_row.at[0],
            halo_send.at[2], halo_recv.at[2], device_id={"row": down_row}, device_id_type=MESH),
        pltpu.make_async_remote_copy(
            x_ref.at[0:tile_cols, 3 * quarter:], halo_row.at[1],
            halo_send.at[3], halo_recv.at[3], device_id={"row": up_row}, device_id_type=MESH),
    ]

    def share_of(c):
        p, part = CHUNKS[c]
        return w_ref.at[p, :, pl.ds(pl.multiple_of(half * half_w + part * cw, cw), cw)]

    def send(c, source, zz, qq, recv, to):
        pltpu.make_async_remote_copy(
            source, wf.at[c, half, zz, qq], w_send.at[c], recv,
            device_id={"row": to}, device_id_type=MESH).start()

    def arrive(ref, recv):
        pltpu.make_async_remote_copy(
            ref, ref, m_send.at[0], recv, device_id={"col": mate}, device_id_type=MESH).wait_recv()

    def left_by(ref, sem):
        pltpu.make_async_remote_copy(
            ref, ref, sem, m_recv.at[0], device_id={"col": mate}, device_id_type=MESH).wait_send()

    def own_copy(c):
        return pltpu.make_async_copy(share_of(c), wf.at[c, half, z, q], own_sem.at[c])

    def own(c):
        for o in range(1, depth):
            send(c, share_of(c), z, q, z_recv.at[c, z], (z + o) % depth * PLANE + q)
        send(c, share_of(c), z, q, s_recv.at[c, 0], second_row)
        send(c, share_of(c), z, q, f_recv.at[c, z], first_row)
        own_copy(c).start()

    def to_mate(c, qq):
        ref = wf.at[c, half, :, qq]
        pltpu.make_async_remote_copy(
            ref, ref, m_send.at[c], m_recv.at[c], device_id={"col": mate}, device_id_type=MESH).start()

    def near(c):
        here = wf.at[c, half, z, q1]
        arrive(here, f_recv.at[c, z])
        send(c, here, z, q1, s_recv.at[c, 1], second_row)

    def planes(c):
        for o in range(1, depth):
            zz = (z + o) % depth
            here = wf.at[c, half, zz, q]
            arrive(here, z_recv.at[c, zz])
            send(c, here, zz, q, s_recv.at[c, 0], second_row)
            send(c, here, zz, q, f_recv.at[c, zz], first_row)
        own_copy(c).wait()
        to_mate(c, q)

    def firsts(c):
        for o in range(1, depth):
            zz = (z + o) % depth
            here = wf.at[c, half, zz, q1]
            arrive(here, f_recv.at[c, zz])
            send(c, here, zz, q1, s_recv.at[c, 1], second_row)
        to_mate(c, q1)

    def seconds(c):
        arrive(wf.at[c, half, :, q2], s_recv.at[c, 0])
        to_mate(c, q2)
        arrive(wf.at[c, half, :, q12], s_recv.at[c, 1])
        to_mate(c, q12)

    def from_mate(c):
        arrive(wf.at[c, 1 - half], m_recv.at[c])

    own(0)
    halos[0].start()
    halos[1].start()

    @pl.when(has_next)
    def _():
        halos[2].start()

    @pl.when(has_previous)
    def _():
        halos[3].start()

    own(1)
    own(2)

    before_c = running_c - ret_c
    before_r = running_r - ret
    total_r = running_c[count - 1:count, :]
    rows_t[0] = running_c
    rows_t[1] = before_c
    chosen = (iota((heads, width), 0) == iota((heads, width), 1) // hd).astype(F32)
    for k, table in enumerate((jnp.exp(total_r - running_c), jnp.exp(before_c))):
        spread_t[k] = jnp.dot(table, chosen, precision=HIGH, preferred_element_type=F32)
    mine[...] = jnp.broadcast_to(
        jnp.concatenate([total_r, jnp.zeros((1, 128 - heads), F32)], axis=1), (8, 128))
    totals[row] = mine[...]

    def picked(table, h):
        return jnp.sum(jnp.where(iota(table.shape, 1) == h, table, 0.0), axis=1, keepdims=True)

    def picked_row(table, h):
        return jnp.sum(jnp.where(iota(table.shape, 0) == h, table, 0.0), axis=0, keepdims=True)

    earlier = iota((count, count), 0) > iota((count, count), 1)
    diagonal = iota((count, count), 0) == iota((count, count), 1)

    def decays(h, carry):
        rc, bc = picked(rows_t[0], h), picked(rows_t[1], h)
        rr, br = picked_row(running_r, h), picked_row(before_r, h)
        exponent = jnp.where(earlier, bc - rr, br - rc)
        decay[h] = jnp.where(diagonal, 0.0, jnp.exp(exponent))
        return carry

    def some_decays(part):
        lax.fori_loop(part * heads // 4, (part + 1) * heads // 4, decays, 0)

    def mix_inputs():
        halos[0].wait()
        halos[1].wait()

        @pl.when(has_next)
        def _():
            halos[2].wait_send()
            halos[3].wait_recv()

        @pl.when(has_previous)
        def _():
            halos[3].wait_send()
            halos[2].wait_recv()

        token = iota((count, quarter), 0)
        place_in_row = token % tile_cols
        x0 = xv[:, 0:quarter].astype(F32)
        x1 = xv[:, quarter:2 * quarter].astype(F32)
        side0 = jnp.where(col > 0, halo_side[0].astype(F32), 0.0)
        side1 = jnp.where(col < cols - 1, halo_side[1].astype(F32), 0.0)
        top = jnp.where(row > 0, halo_row[0].astype(F32), 0.0)
        bottom = jnp.where(row < rows - 1, halo_row[1].astype(F32), 0.0)
        last = tile_cols - 1
        shifted = [
            jnp.where(place_in_row == 0, pltpu.roll(side0, count - last, 0), pltpu.roll(x0, 1, 0)),
            jnp.where(place_in_row == last, pltpu.roll(side1, last, 0), pltpu.roll(x1, count - 1, 0)),
            jnp.concatenate([top, xv[0:count - tile_cols, 2 * quarter:3 * quarter].astype(F32)], axis=0),
            jnp.concatenate([xv[tile_cols:count, 3 * quarter:].astype(F32), bottom], axis=0),
        ]
        for part in range(4):
            span = slice(part * quarter, (part + 1) * quarter)
            xs = xv[:, span].astype(F32)
            for p in range(3):
                c = ratio_ref[p:p + 1, span]
                mx[p, :, span] = (xs * c + shifted[part] * (1.0 - c)).astype(BF16)

    def project(c):
        p, part = CHUNKS[c]

        def one(side, carry):
            dst = pl.ds(pl.multiple_of(side * half_w + part * cw, cw), cw)
            proj[p, :, dst] = jnp.dot(
                mx[p], wf[c, side].reshape(width, cw), preferred_element_type=F32).astype(BF16)
            return carry

        lax.fori_loop(0, 2, one, 0)

    lane = iota((count, lanes), 1)
    low = lane < hd
    low_u = iota((hd, lanes), 1) < hd
    same_head = (iota((2 * lanes, lanes), 0) % lanes // hd == iota((2 * lanes, lanes), 1) // hd).astype(BF16)

    def halves(value):
        return jnp.dot(jnp.concatenate(two_terms(value), axis=1), same_head, preferred_element_type=F32)

    def pair_of(u, j):
        return j // side_pairs * (pairs // 2) + u * side_pairs + j % side_pairs

    def span_of(i):
        return pl.ds(pl.multiple_of(i * lanes, lanes), lanes)

    def local_states(u):
        def one(j, carry):
            span = span_of(pair_of(u, j))
            k = proj[1, :, span].astype(F32)
            v = proj[2, :, span]
            kd = jnp.concatenate([k * spread_t[0, :, span], k * spread_t[1, :, span]], axis=1).astype(BF16)
            m = lax.dot_general(kd, v, (((0,), (0,)), ((), ())), preferred_element_type=F32)
            a = jnp.where(low_u, m[0:hd], pltpu.roll(m[2 * hd:3 * hd], hd, 1))
            b = jnp.where(low_u, pltpu.roll(m[hd:2 * hd], hd, 1), m[3 * hd:])
            for s in range(per):
                states[u, 2 * j * per + s] = a[s * unit:(s + 1) * unit].astype(BF16)
                states[u, (2 * j + 1) * per + s] = b[s * unit:(s + 1) * unit].astype(BF16)
            return carry

        lax.fori_loop(0, group_pairs, one, 0)

    def to_all(copy):
        def one(o, carry):
            copy((row + o) % rows).start()
            return carry

        lax.fori_loop(1, rows, one, 0)

    def totals_out():
        to_all(lambda to: pltpu.make_async_remote_copy(
            mine, totals.at[row], t_send, t_recv, device_id={"row": to}, device_id_type=MESH))

    def states_out(u):
        to_all(lambda to: pltpu.make_async_remote_copy(
            states.at[u, to], arrived.at[u, row], a_send.at[u], a_recv.at[u],
            device_id={"row": to}, device_id_type=MESH))
        arrived[u, row] = states[u, row]

    def totals_in():
        arrive(totals.at[0:rows - 1], t_recv)
        everyone = totals[...]
        for u in range(SPLIT):
            local = row * unit // hd
            head = 2 * pair_of(u, local // 2) + local % 2
            here = iota(everyone.shape, 2) == head
            kept_all[u] = jnp.broadcast_to(
                jnp.exp(jnp.sum(jnp.where(here, everyone, 0.0), axis=2, keepdims=True)), everyone.shape)

    def scan(u):
        arrive(arrived.at[u, 0:rows - 1], a_recv.at[u])

        def one(j, carry):
            ahead, behind = carry
            back = rows - 1 - j
            scan_f[j] = ahead
            scan_b[back] = behind
            ahead = kept_all[u, j][0:1, :] * ahead + arrived[u, j].astype(F32)
            behind = kept_all[u, back][0:1, :] * behind + arrived[u, back].astype(F32)
            return ahead, behind

        start = jnp.zeros((unit, lanes), F32)
        lax.fori_loop(0, rows, one, (start, start), unroll=4)
        leaving[u] = jnp.where(iota(scan_f.shape, 2) < hd, scan_f[...], scan_b[...]).astype(BF16)
        to_all(lambda to: pltpu.make_async_remote_copy(
            leaving.at[u, to], entering.at[u, row], b_send.at[u], b_recv.at[u],
            device_id={"row": to}, device_id_type=MESH))
        entering[u, row] = leaving[u, row]

    def local_mix(u):
        def one(j, carry):
            i = pair_of(u, j)
            span = span_of(i)
            r, k, v = proj[0, :, span], proj[1, :, span], proj[2, :, span]
            outs = []
            for s in range(2):
                rs = jnp.where(low if s == 0 else jnp.logical_not(low), r.astype(F32), 0.0).astype(BF16)
                scores = lax.dot_general(rs, k, contract_last, preferred_element_type=F32)
                weight = (scores * decay[2 * i + s]).astype(BF16)
                outs.append(jnp.dot(weight, v, preferred_element_type=F32))
            own_term = halves(r.astype(F32) * credit_ref[:, span] * k.astype(F32)) * v.astype(F32)
            block[i] = jnp.where(low, outs[0], outs[1]) + own_term
            return carry

        lax.fori_loop(0, group_pairs, one, 0)

    def finish(u, total):
        arrive(entering.at[u, 0:rows - 1], b_recv.at[u])

        def one(j, total):
            i = pair_of(u, j)
            span = span_of(i)
            r = proj[0, :, span]
            a = jnp.concatenate([entering[u, 2 * j * per + s].astype(F32) for s in range(per)], axis=0)
            b = jnp.concatenate([entering[u, (2 * j + 1) * per + s].astype(F32) for s in range(per)], axis=0)
            fwd = jnp.concatenate(
                [jnp.where(low_u, a, 0.0), jnp.where(low_u, 0.0, pltpu.roll(b, hd, 1))], axis=0).astype(BF16)
            bwd = jnp.concatenate(
                [jnp.where(low_u, pltpu.roll(a, hd, 1), 0.0), jnp.where(low_u, 0.0, b)], axis=0).astype(BF16)
            wkv = (
                block[i]
                + spread_t[1, :, span] * jnp.dot(r, fwd, preferred_element_type=F32)
                + spread_t[0, :, span] * jnp.dot(r, bwd, preferred_element_type=F32)
            )
            centred = wkv - halves(wkv) * (1.0 / hd)
            variance = halves(centred * centred) * (1.0 / hd)
            made = xv[:, span].astype(F32) + centred * lax.rsqrt(variance + 1e-05) * gain_ref[:, span]
            block[i] = made
            return total + made

        return lax.fori_loop(0, group_pairs, one, total)

    near(0)
    planes(0)
    x_copy.wait()
    mix_inputs()
    own(3)
    near(1)
    planes(1)
    firsts(0)
    some_decays(0)
    some_decays(1)
    own(4)
    near(2)
    planes(2)
    firsts(1)
    seconds(0)
    totals_out()
    some_decays(2)
    some_decays(3)
    own(5)
    near(3)
    planes(3)
    firsts(2)
    seconds(1)
    from_mate(0)
    project(0)
    totals_in()
    near(4)
    planes(4)
    firsts(3)
    from_mate(1)
    project(1)
    local_states(0)
    states_out(0)
    seconds(2)
    near(5)
    planes(5)
    firsts(4)
    seconds(3)
    from_mate(2)
    project(2)
    scan(0)
    firsts(5)
    from_mate(3)
    project(3)
    local_states(1)
    states_out(1)
    seconds(4)
    from_mate(4)
    project(4)
    local_mix(0)
    scan(1)
    seconds(5)
    total = finish(0, jnp.zeros((count, lanes), F32))
    from_mate(5)
    project(5)
    local_mix(1)
    total = finish(1, total)

    group = (
        (iota((count, count), 0) // (2 * tile_cols) == iota((count, count), 1) // (2 * tile_cols))
        & (iota((count, count), 0) % tile_cols // 2 == iota((count, count), 1) % tile_cols // 2)
    ).astype(BF16)

    def over_group(value):
        rowsum = jnp.broadcast_to(jnp.sum(value, axis=1, keepdims=True), (count, lanes))
        both = jnp.dot(group, jnp.concatenate(two_terms(rowsum), axis=1), preferred_element_type=F32)
        return (both[:, 0:lanes] + both[:, lanes:]) * (1.0 / (4 * width))

    mean = over_group(total)

    def spread(i, acc):
        dev = block[i] - mean
        return acc + dev * dev

    variance = over_group(lax.fori_loop(0, pairs, spread, jnp.zeros((count, lanes), F32)))
    stats[0] = mean
    stats[1] = lax.rsqrt(variance + 1e-05)
    half_cols = tile_cols // 2

    def emit(i, carry):
        for part in range(4):
            span = pl.ds(pl.multiple_of(part * width + i * lanes, lanes), lanes)
            g, o = scale_ref[:, span], offset_ref[:, span]
            for a in range(tile_rows // 2):
                take = pl.ds((2 * a + part % 2) * tile_cols + part // 2, half_cols, stride=2)
                value = (block[i, take, :] - stats[0, take, :]) * stats[1, take, :]
                out_ref[a, :, span] = (value * g + o).astype(BF16)
        return carry

    lax.fori_loop(0, pairs, emit, 0)

    left_by(totals.at[0:rows - 1], t_send)
    for u in range(SPLIT):
        left_by(states.at[u, 0:rows - 1], a_send.at[u])
        left_by(leaving.at[u, 0:rows - 1], b_send.at[u])
    for c in range(len(CHUNKS)):
        left_by(wf.at[c, half], m_send.at[c])
        left_by(wf.at[c, half, 0:depth - 1], w_send.at[c])
        left_by(wf.at[c, half, 0, 0:PLANE - 1], w_send.at[c])


def body(x, ratios, w, retention, credit, gain, scale, offset):
    tile_rows, tile_cols, width = x.shape
    heads = retention.shape[0]
    count = tile_rows * tile_cols
    hd = width // heads
    rows, cols = lax.axis_size("row"), lax.axis_size("col")
    depth = rows // PLANE
    unit = heads * hd // rows // SPLIT
    pairs = heads // 2
    lanes = 2 * hd
    chunks = len(CHUNKS)
    dma = pltpu.SemaphoreType.DMA
    anywhere, vmem = pl.BlockSpec(memory_space=pl.ANY), pl.BlockSpec(memory_space=pltpu.VMEM)
    return pl.pallas_call(
        functools.partial(kernel, rows, cols, tile_rows, tile_cols, heads),
        out_shape=jax.ShapeDtypeStruct((tile_rows // 2, tile_cols // 2, 4 * width), BF16),
        in_specs=[anywhere, vmem, anywhere, vmem, vmem, vmem, vmem, vmem],
        out_specs=vmem,
        scratch_shapes=[
            pltpu.VMEM((count, width), BF16),
            pltpu.VMEM((chunks, 2, depth, PLANE, w.shape[1], width // 2 // SPLIT), BF16),
            pltpu.VMEM((3, count, width), BF16),
            pltpu.VMEM((3, count, width), BF16),
            pltpu.VMEM((heads, count, count), F32),
            pltpu.VMEM((2, count, width // 4), BF16),
            pltpu.VMEM((2, tile_cols, width // 4), BF16),
            pltpu.VMEM((2, count, heads), F32),
            pltpu.VMEM((2, count, width), F32),
            pltpu.VMEM((8, 128), F32),
            pltpu.VMEM((rows, 8, 128), F32),
            pltpu.VMEM((SPLIT, rows, 8, 128), F32),
            pltpu.VMEM((SPLIT, rows, unit, lanes), BF16),
            pltpu.VMEM((SPLIT, rows, unit, lanes), BF16),
            pltpu.VMEM((rows, unit, lanes), F32),
            pltpu.VMEM((rows, unit, lanes), F32),
            pltpu.VMEM((SPLIT, rows, unit, lanes), BF16),
            pltpu.VMEM((SPLIT, rows, unit, lanes), BF16),
            pltpu.VMEM((pairs, count, lanes), F32),
            pltpu.VMEM((2, count, lanes), F32),
            dma,
            dma((chunks,)),
            dma((chunks,)),
            dma((chunks,)),
            dma((chunks, depth)),
            dma((chunks, depth)),
            dma((chunks, 2)),
            dma((chunks,)),
            dma((4,)),
            dma((4,)),
            dma,
            dma,
            dma((SPLIT,)),
            dma((SPLIT,)),
            dma((SPLIT,)),
            dma((SPLIT,)),
        ],
        compiler_params=pltpu.CompilerParams(
            collective_id=0, has_side_effects=True, vmem_limit_bytes=60 * 1024 * 1024),
    )(
        x.reshape(count, width), ratios, w, retention,
        credit.reshape(1, width), gain.reshape(1, width),
        scale.reshape(1, 4 * width), offset.reshape(1, 4 * width),
    )


def solution(mesh):
    return jax.shard_map(
        body,
        mesh=mesh,
        in_specs=(
            P("row", "col", None),
            P(),
            P(None, "row", None),
            P(None, "row", "col"),
            P(),
            P(),
            P(),
            P(),
        ),
        out_specs=P("row", "col", None),
        check_vma=False,
    )
```

time: 67.1 us -> 57.1 us (0.85)
  Pallas kernels: 65 us -> 55 us
    pallas_call x1, Pallas kernels: 65 us -> 55 us  [body(): pl.pallas_call(functools.partial(kernel, rows, cols, tile_rows, tile_cols...]
where the time goes in v1:
time: 57.1 us; the launch traced here: 56.9 us
  Pallas kernels  55 us (96%)
  local copies, waits for them, and re-layouts  1.87 us (3%)
    pallas_call x1, Pallas kernels, body(): pl.pallas_call(functools.partial(kernel, rows, cols, tile_rows, tile_cols...  55 us
    unnamed x1, local copies, waits for them, and re-layouts  1.87 us

profile of v1, /device:TPU:0, one launch (start us, length us, event | category | flops | bytes accessed | tf_op | source)
XLA Modules:
  0.0 56.9 jit_solution(17845029695168134290)
XLA Ops:
  0.0 55.0 %shard_map.82 = bf16[4,16,4096]{2,1,0:T(8,128)(2,1)} custom-call(bf16[256,1024]{1,0:T(8,128)(2,1)} %bitcast.5, f32[3,1024]{1,0:T(4,128)} %ratio_ref.1, bf16[3,64,1024]{2,1,0:T(8,128)(2,1)} %w_ref.1, f32[16,8,32]{2,1,0:T(8,128)} %ret_ref.1, f32[1,1024]{1,0:T(1,128)} %bitcast.8, f32[1,1024]{1,0:T(1,128)} %bitcast.9, f32[1,4096]{1,0:T(1,128)} %bitcast.6, ...), custom_call_target="tpu_custom_call" | custom-call | tf_op jit(solution)/shard_map/pallas_call | solution.py:499
  55.0 1.9 %copy.10 = bf16[4,16,4096]{2,1,0:T(8,128)(2,1)} copy(bf16[4,16,4096]{2,1,0:T(8,128)(2,1)} %shard_map.82) | data formatting | bytes 1048576

commit v2 on v1

v2 whole, which is shorter than its diff:
```python
import functools

import jax
import jax.numpy as jnp
from jax import lax
from jax.experimental import pallas as pl
from jax.experimental.pallas import tpu as pltpu
from jax.sharding import PartitionSpec as P

MESH = pl.DeviceIdType.MESH
F32 = jnp.float32
BF16 = jnp.bfloat16
HIGH = lax.Precision.HIGHEST
PLANE = 4
PIECES = 4
KV, R = slice(1, 3), slice(0, 1)


def iota(shape, dim):
    return lax.broadcasted_iota(jnp.int32, shape, dim)


def two_terms(value):
    first = value.astype(BF16)
    return first, (value - first.astype(F32)).astype(BF16)


def kernel(
    rows, cols, tile_rows, tile_cols, heads,
    x_ref, ratio_ref, w_ref, ret_ref, credit_ref, gain_ref, scale_ref, offset_ref,
    out_ref,
    xt, wf, mx, proj, decay, side, top_rows, bottom_rows, rets, rows_t, rows_r, spread_t, log_t, plane_log, plane_logs,
    sums, before, decays_t, plane_sum, plane_sums, entering, block, sent, landed, stats,
    x_own, x_send, x_piece, x_near, x_far, w_own, w_send, w_plane, w_z, w_mate, side_send, side_recv, edge_own,
    edge_send, edge_recv, ret_send, ret_recv, log_send, log_recv, sum_send, sum_recv, out_send, out_recv,
):
    count, width = xt.shape[1:]
    hd = width // heads
    lanes = 2 * hd
    quarter = width // 4
    gw = width // PLANE
    gp = gw // lanes
    hp = heads // PLANE
    vp_count = PLANE * gp
    hs = w_ref.shape[1] // 2
    piece = count // PIECES
    row, col = lax.axis_index("row"), lax.axis_index("col")
    depth = rows // PLANE
    z, q = row // PLANE, row % PLANE
    bx, by = q % 2, q // 2
    half = col % 2
    mate = col + 1 - 2 * half
    q1 = (1 - half) * (q + 1 - 2 * bx) + half * (q + 2 - 4 * by)
    q2 = half * (q + 1 - 2 * bx) + (1 - half) * (q + 2 - 4 * by)
    q12 = PLANE - 1 - q
    base = z * PLANE
    first_row, second_row = base + q1, base + q2
    right, left = (col + 1) % cols, (col + cols - 1) % cols
    sends_down = (q < PLANE - 1) | (z < depth - 1)
    sends_up = (q > 0) | (z > 0)
    down_plane = jnp.where(q < PLANE - 1, z, (z + 1) % depth)
    up_plane = jnp.where(q > 0, z, (z + depth - 1) % depth)
    down_slot, up_slot = (q + 1) % PLANE, (q + PLANE - 1) % PLANE

    barrier = pltpu.get_barrier_semaphore()

    def greet(target):
        pl.semaphore_signal(barrier, inc=1, device_id=target, device_id_type=MESH)

    for o in range(1, depth):
        greet({"row": (z + o) % depth * PLANE + q})
    for o in range(1, PLANE):
        greet({"row": base + (q + o) % PLANE})
    for other in (right, left, mate):
        greet({"col": other})

    @pl.when(z > 0)
    def _():
        greet({"row": (base + rows - 1) % rows})

    @pl.when(z < depth - 1)
    def _():
        greet({"row": (base + PLANE) % rows})

    def local(src, dst, sem):
        return pltpu.make_async_copy(src, dst, sem)

    def remote(src, dst, send, recv, target):
        return pltpu.make_async_remote_copy(
            src, dst, send, recv, device_id=target, device_id_type=MESH)

    def arrive(ref, recv):
        remote(ref, ref, x_send, recv, {"col": mate}).wait_recv()

    def left_by(ref, send):
        remote(ref, ref, send, x_near, {"col": mate}).wait_send()

    my_rows = pl.ds(pl.multiple_of(half * hs, hs), hs)

    def my_cols(qq):
        return pl.ds(pl.multiple_of(qq * gw, gw), gw)

    x_copy = local(x_ref, xt.at[q], x_own)
    w_copy = local(w_ref.at[:, my_rows, my_cols(q)], wf.at[:, z, q, half], w_own)
    w_copy.start()
    x_copy.start()
    top_source = x_ref.at[count - tile_cols:count, 2 * quarter:3 * quarter]
    bottom_source = x_ref.at[0:tile_cols, 3 * quarter:]
    rets[q] = jnp.concatenate([ret_ref[:, r, :] for r in range(tile_rows)], axis=1)

    expected = (
        depth + PLANE + 1
        + PLANE * ((q == PLANE - 1) & (z < depth - 1)).astype(jnp.int32)
        + PLANE * ((q == 0) & (z > 0)).astype(jnp.int32)
    )
    pl.semaphore_wait(barrier, expected)

    def weights_to_plane(which, k):
        for o in range(1, PLANE):
            qq = (q + o) % PLANE
            remote(
                w_ref.at[which, my_rows, my_cols(qq)], wf.at[which, z, q, half], w_send.at[0], w_plane.at[k],
                {"row": base + qq}).start()

    def side_copies(t, source):
        return [
            remote(source.at[:, 0:quarter], side.at[t, 0], side_send.at[t, 0], side_recv.at[t, 0], {"col": right}),
            remote(source.at[:, quarter:2 * quarter], side.at[t, 1], side_send.at[t, 1], side_recv.at[t, 1],
                   {"col": left}),
        ]

    def edges(act):
        for qq in range(PLANE):
            to = down_plane * PLANE + qq

            @pl.when(sends_down & (to != row))
            def _():
                act(remote(top_source, top_rows.at[down_slot], edge_send.at[0, qq], edge_recv.at[0, down_slot],
                           {"row": to}))

            to_up = up_plane * PLANE + qq

            @pl.when(sends_up & (to_up != row))
            def _():
                act(remote(bottom_source, bottom_rows.at[up_slot], edge_send.at[1, qq], edge_recv.at[1, up_slot],
                           {"row": to_up}))

    top_own = local(top_source, top_rows.at[down_slot], edge_own.at[0])
    bottom_own = local(bottom_source, bottom_rows.at[up_slot], edge_own.at[1])

    def own_edges(act):
        @pl.when(q < PLANE - 1)
        def _():
            act(top_own)

        @pl.when(q > 0)
        def _():
            act(bottom_own)

    weights_to_plane(KV, 0)
    for o in range(1, PLANE):
        remote(rets.at[q], rets.at[q], ret_send, ret_recv, {"row": base + (q + o) % PLANE}).start()
    edges(lambda c: c.start())
    own_edges(lambda c: c.start())
    for c in side_copies(q, x_ref):
        c.start()
    for k in range(PIECES):
        part = slice(k * piece, (k + 1) * piece)
        remote(x_ref.at[part], xt.at[q, part], x_send, x_piece.at[k], {"row": first_row}).start()
    remote(x_ref, xt.at[q], x_send, x_near, {"row": second_row}).start()
    weights_to_plane(R, 1)

    def weights_to_mate(which, k, zz):
        here = wf.at[which, zz, :, half]
        remote(here, here, w_send.at[2], w_mate.at[k], {"col": mate}).start()

    def weights_along_z(which, k):
        arrive(wf.at[which, z, 0:PLANE - 1, half], w_plane.at[k])
        here = wf.at[which, z, :, half]
        for o in range(1, depth):
            remote(here, here, w_send.at[1], w_z.at[k, z], {"row": (z + o) % depth * PLANE + q}).start()
        weights_to_mate(which, k, z)

    def weights_from_z(which, k):
        for o in range(1, depth):
            zz = (z + o) % depth
            arrive(wf.at[which, zz, :, half], w_z.at[k, zz])
            weights_to_mate(which, k, zz)

    def weights_from_mate(which, k):
        arrive(wf.at[which, :, :, 1 - half], w_mate.at[k])

    w_copy.wait()
    weights_along_z(KV, 0)

    arrive(rets.at[0:PLANE - 1], ret_recv)
    all_rets = jnp.concatenate([rets[t] for t in range(PLANE)], axis=0)
    picks = (
        iota((heads, PLANE * heads), 1)
        == iota((heads, PLANE * heads), 0) // hp * heads + q * hp + iota((heads, PLANE * heads), 0) % hp
    ).astype(F32)
    ret = jnp.dot(picks, all_rets, precision=HIGH, preferred_element_type=F32)
    tri = (iota((count, count), 0) >= iota((count, count), 1)).astype(F32)
    contract_last = (((1,), (1,)), ((), ()))
    running_c = lax.dot_general(tri, ret, contract_last, precision=HIGH, preferred_element_type=F32)
    running_r = lax.dot_general(ret, tri, contract_last, precision=HIGH, preferred_element_type=F32)
    eye = (iota((count, count), 0) == iota((count, count), 1)).astype(F32)
    ret_c = lax.dot_general(eye, ret, contract_last, precision=HIGH, preferred_element_type=F32)
    before_c = running_c - ret_c
    total_r = running_c[count - 1:count, :]
    rows_t[0] = running_c
    rows_t[1] = before_c
    rows_r[0] = running_r
    rows_r[1] = running_r - ret
    chosen = (iota((heads, width), 0) == iota((heads, width), 1) // hd).astype(F32)
    for k, table in enumerate((jnp.exp(total_r - running_c), jnp.exp(before_c))):
        spread_t[k] = jnp.dot(table, chosen, precision=HIGH, preferred_element_type=F32)
    log_t[...] = jnp.dot(jnp.broadcast_to(total_r, (8, heads)), chosen, precision=HIGH, preferred_element_type=F32)

    def log_of(vp):
        return log_t[:, vp * lanes:(vp + 1) * lanes]

    for j in range(gp):
        plane_log[j] = sum(log_of(t * gp + j) for t in range(PLANE))
    for o in range(1, depth):
        remote(plane_log, plane_logs.at[z], log_send, log_recv, {"row": (z + o) % depth * PLANE + q}).start()
    for j in range(gp):
        for t in range(PLANE):
            vp = t * gp + j
            zero = jnp.zeros((8, lanes), F32)
            decays_t[0, vp] = jnp.exp(log_of(vp))
            decays_t[1, vp] = jnp.exp(sum((log_of(s * gp + j) for s in range(t)), zero))
            decays_t[2, vp] = jnp.exp(sum((log_of(s * gp + j) for s in range(t + 1, PLANE)), zero))

    def picked(table, h):
        return jnp.sum(jnp.where(iota(table.shape, 1) == h, table, 0.0), axis=1, keepdims=True)

    def picked_row(table, h):
        return jnp.sum(jnp.where(iota(table.shape, 0) == h, table, 0.0), axis=0, keepdims=True)

    earlier = iota((count, count), 0) > iota((count, count), 1)
    diagonal = iota((count, count), 0) == iota((count, count), 1)

    def pair_decays(h, carry):
        rc, bc = picked(rows_t[0], h), picked(rows_t[1], h)
        rr, br = picked_row(rows_r[0], h), picked_row(rows_r[1], h)
        exponent = jnp.where(earlier, bc - rr, br - rc)
        decay[h] = jnp.where(diagonal, 0.0, jnp.exp(exponent))
        return carry

    def some_decays(part):
        lax.fori_loop(part * heads // 4, (part + 1) * heads // 4, pair_decays, 0)

    def forward(k):
        part = slice(k * piece, (k + 1) * piece)
        here = xt.at[q1, part]
        arrive(here, x_piece.at[k])
        remote(here, here, x_send, x_far, {"row": second_row}).start()

    def sides_out(t):
        for c in side_copies(t, xt.at[t]):
            c.start()

    def edges_in():
        own_edges(lambda c: c.wait())
        for t in range(PLANE):
            @pl.when((base + t > 0) & (q != t - 1))
            def _():
                arrive(top_rows.at[t], edge_recv.at[0, t])

            @pl.when((base + t < rows - 1) & (q != t + 1))
            def _():
                arrive(bottom_rows.at[t], edge_recv.at[1, t])

    place_in_row = iota((count, quarter), 0) % tile_cols
    last = tile_cols - 1

    def mix(t):
        for c in side_copies(t, xt.at[t]):
            c.wait_recv()
        x0 = xt[t, :, 0:quarter].astype(F32)
        x1 = xt[t, :, quarter:2 * quarter].astype(F32)
        side0 = jnp.where(col > 0, side[t, 0].astype(F32), 0.0)
        side1 = jnp.where(col < cols - 1, side[t, 1].astype(F32), 0.0)
        top = jnp.where(base + t > 0, top_rows[t].astype(F32), 0.0)
        bottom = jnp.where(base + t < rows - 1, bottom_rows[t].astype(F32), 0.0)
        shifted = [
            jnp.where(place_in_row == 0, pltpu.roll(side0, count - last, 0), pltpu.roll(x0, 1, 0)),
            jnp.where(place_in_row == last, pltpu.roll(side1, last, 0), pltpu.roll(x1, count - 1, 0)),
            jnp.concatenate([top, xt[t, 0:count - tile_cols, 2 * quarter:3 * quarter].astype(F32)], axis=0),
            jnp.concatenate([xt[t, tile_cols:count, 3 * quarter:].astype(F32), bottom], axis=0),
        ]
        for part in range(4):
            span = slice(part * quarter, (part + 1) * quarter)
            xs = xt[t, :, span].astype(F32)
            for p in range(3):
                c = ratio_ref[p:p + 1, span]
                mx[t, p, :, span] = (xs * c + shifted[part] * (1.0 - c)).astype(BF16)

    def project(p, t):
        proj[p, :, my_cols(t)] = jnp.dot(
            mx[t, p], wf[p].reshape(width, gw), preferred_element_type=F32).astype(BF16)

    low = iota((count, lanes), 1) < hd
    low_u = iota((hd, lanes), 1) < hd
    same_head = (iota((2 * lanes, lanes), 0) % lanes // hd == iota((2 * lanes, lanes), 1) // hd).astype(BF16)

    def halves(value):
        return jnp.dot(jnp.concatenate(two_terms(value), axis=1), same_head, preferred_element_type=F32)

    def span_of(i):
        return pl.ds(pl.multiple_of(i * lanes, lanes), lanes)

    def local_states(t):
        def one(j, carry):
            vp = t * gp + j
            span = span_of(vp)
            k = proj[1, :, span].astype(F32)
            v = proj[2, :, span]
            kd = jnp.concatenate([k * spread_t[0, :, span], k * spread_t[1, :, span]], axis=1).astype(BF16)
            m = lax.dot_general(kd, v, (((0,), (0,)), ((), ())), preferred_element_type=F32)
            sums[0, vp] = jnp.where(low_u, m[0:hd], m[hd:2 * hd])
            sums[1, vp] = jnp.where(low_u, m[2 * hd:3 * hd], m[3 * hd:])
            return carry

        lax.fori_loop(0, gp, one, 0)

    def keys_values(t):
        project(1, t)
        project(2, t)
        local_states(t)

    def planes_out():
        for j in range(gp):
            for d, order in ((0, range(PLANE)), (1, range(PLANE - 1, -1, -1))):
                state = jnp.zeros((hd, lanes), F32)
                for t in order:
                    vp = t * gp + j
                    before[d, vp] = state
                    state = decays_t[0, vp][0:1, :] * state + sums[d, vp]
                plane_sum[d, j] = state.astype(BF16)
        for o in range(1, depth):
            zz = (z + o) % depth
            remote(
                plane_sum.at[(zz < z).astype(jnp.int32)], plane_sums.at[z], sum_send, sum_recv,
                {"row": zz * PLANE + q}).start()

    def planes_in():
        arrive(plane_logs.at[0:depth - 1], log_recv)
        arrive(plane_sums.at[0:depth - 1], sum_recv)
        for j in range(gp):
            def one(i, carry):
                fwd, bwd = carry
                back = depth - 1 - i
                fwd = jnp.where(
                    i < z, jnp.exp(plane_logs[i, j][0:1, :]) * fwd + plane_sums[i, j].astype(F32), fwd)
                bwd = jnp.where(
                    back > z, jnp.exp(plane_logs[back, j][0:1, :]) * bwd + plane_sums[back, j].astype(F32), bwd)
                return fwd, bwd

            start = jnp.zeros((hd, lanes), F32)
            reached = lax.fori_loop(0, depth, one, (start, start), unroll=True if depth <= 4 else 1)
            for t in range(PLANE):
                vp = t * gp + j
                for d in range(2):
                    entering[d, vp] = before[d, vp] + decays_t[1 + d, vp][0:1, :] * reached[d]

    def channels(j):
        return pl.ds(pl.multiple_of(q * gw + j * lanes, lanes), lanes)

    def local_mix(t):
        def one(j, carry):
            vp = t * gp + j
            span = span_of(vp)
            r, k, v = proj[0, :, span], proj[1, :, span], proj[2, :, span]
            outs = []
            for s in range(2):
                rs = jnp.where(low if s == 0 else jnp.logical_not(low), r.astype(F32), 0.0).astype(BF16)
                scores = lax.dot_general(rs, k, contract_last, preferred_element_type=F32)
                weight = (scores * decay[2 * vp + s]).astype(BF16)
                outs.append(jnp.dot(weight, v, preferred_element_type=F32))
            own_term = halves(r.astype(F32) * credit_ref[:, channels(j)] * k.astype(F32)) * v.astype(F32)
            block[vp] = jnp.where(low, outs[0], outs[1]) + own_term
            return carry

        lax.fori_loop(0, gp, one, 0)

    def finish(t, dst):
        def one(j, carry):
            vp = t * gp + j
            span = span_of(vp)
            r = proj[0, :, span]
            fwd, bwd = [
                jnp.concatenate(
                    [jnp.where(low_u, entering[d, vp], 0.0), jnp.where(low_u, 0.0, entering[d, vp])], axis=0
                ).astype(BF16)
                for d in range(2)
            ]
            wkv = (
                block[vp]
                + spread_t[1, :, span] * jnp.dot(r, fwd, preferred_element_type=F32)
                + spread_t[0, :, span] * jnp.dot(r, bwd, preferred_element_type=F32)
            )
            centred = wkv - halves(wkv) * (1.0 / hd)
            variance = halves(centred * centred) * (1.0 / hd)
            normed = centred * lax.rsqrt(variance + 1e-05) * gain_ref[:, channels(j)]
            dst[t, :, span_of(j)] = normed.astype(BF16)
            return carry

        lax.fori_loop(0, gp, one, 0)

    def finish_and_send(t):
        finish(t, sent)
        remote(sent.at[t], landed.at[q], out_send, out_recv, {"row": base + t}).start()

    some_decays(0)
    x_copy.wait()
    edges_in()
    forward(0)
    mix(q)
    forward(1)
    some_decays(1)
    forward(2)
    some_decays(2)
    weights_from_z(KV, 0)
    forward(3)
    sides_out(q1)
    weights_along_z(R, 1)
    some_decays(3)
    arrive(xt.at[q2], x_near)
    sides_out(q2)
    weights_from_mate(KV, 0)
    keys_values(q)
    mix(q1)
    keys_values(q1)
    mix(q2)
    keys_values(q2)
    arrive(xt.at[q12], x_far)
    sides_out(q12)
    weights_from_z(R, 1)
    mix(q12)
    keys_values(q12)
    planes_out()
    weights_from_mate(R, 1)
    project(0, q1)
    local_mix(q1)
    project(0, q2)
    local_mix(q2)
    planes_in()
    finish_and_send(q1)
    finish_and_send(q2)
    project(0, q12)
    local_mix(q12)
    finish_and_send(q12)
    project(0, q)
    local_mix(q)
    finish(q, landed)
    arrive(landed.at[0:PLANE - 1], out_recv)

    group = (
        (iota((count, count), 0) // (2 * tile_cols) == iota((count, count), 1) // (2 * tile_cols))
        & (iota((count, count), 0) % tile_cols // 2 == iota((count, count), 1) % tile_cols // 2)
    ).astype(BF16)

    def over_group(value):
        rowsum = jnp.broadcast_to(jnp.sum(value, axis=1, keepdims=True), (count, lanes))
        both = jnp.dot(group, jnp.concatenate(two_terms(rowsum), axis=1), preferred_element_type=F32)
        return (both[:, 0:lanes] + both[:, lanes:]) * (1.0 / (4 * width))

    def add_up(i, total):
        made = xt[q, :, span_of(i)].astype(F32) + landed[i // gp, :, span_of(i % gp)].astype(F32)
        block[i] = made
        return total + made

    none = jnp.zeros((count, lanes), F32)
    mean = over_group(lax.fori_loop(0, vp_count, add_up, none))

    def spread(i, acc):
        dev = block[i] - mean
        return acc + dev * dev

    variance = over_group(lax.fori_loop(0, vp_count, spread, none))
    stats[0] = mean
    stats[1] = lax.rsqrt(variance + 1e-05)
    half_cols = tile_cols // 2

    def emit(i, carry):
        for part in range(4):
            span = pl.ds(pl.multiple_of(part * width + i * lanes, lanes), lanes)
            g, o = scale_ref[:, span], offset_ref[:, span]
            for a in range(tile_rows // 2):
                take = pl.ds((2 * a + part % 2) * tile_cols + part // 2, half_cols, stride=2)
                value = (block[i, take, :] - stats[0, take, :]) * stats[1, take, :]
                out_ref[a, :, span] = (value * g + o).astype(BF16)
        return carry

    lax.fori_loop(0, vp_count, emit, 0)

    left_by(xt.at[0:3], x_send)
    left_by(wf.at[:, z, 0:PLANE - 1, half], w_send.at[0])
    left_by(wf.at[:, 0:depth - 1, :, half], w_send.at[1])
    left_by(wf.at[:, :, :, half], w_send.at[2])
    left_by(rets.at[0:PLANE - 1], ret_send)
    left_by(plane_logs.at[0:depth - 1], log_send)
    left_by(plane_sums.at[0:depth - 1], sum_send)
    left_by(sent.at[0:PLANE - 1], out_send)
    edges(lambda c: c.wait_send())
    for t in range(PLANE):
        for c in side_copies(t, xt.at[t]):
            c.wait_send()


def body(x, ratios, w, retention, credit, gain, scale, offset):
    tile_rows, tile_cols, width = x.shape
    heads = retention.shape[0]
    count = tile_rows * tile_cols
    hd = width // heads
    rows, cols = lax.axis_size("row"), lax.axis_size("col")
    depth = rows // PLANE
    pairs = heads // 2
    lanes = 2 * hd
    gw = width // PLANE
    gp = gw // lanes
    dma = pltpu.SemaphoreType.DMA
    anywhere, vmem = pl.BlockSpec(memory_space=pl.ANY), pl.BlockSpec(memory_space=pltpu.VMEM)
    return pl.pallas_call(
        functools.partial(kernel, rows, cols, tile_rows, tile_cols, heads),
        out_shape=jax.ShapeDtypeStruct((tile_rows // 2, tile_cols // 2, 4 * width), BF16),
        in_specs=[anywhere, vmem, anywhere, vmem, vmem, vmem, vmem, vmem],
        out_specs=vmem,
        scratch_shapes=[
            pltpu.VMEM((PLANE, count, width), BF16),
            pltpu.VMEM((3, depth, PLANE, 2, w.shape[1] // 2, gw), BF16),
            pltpu.VMEM((PLANE, 3, count, width), BF16),
            pltpu.VMEM((3, count, width), BF16),
            pltpu.VMEM((heads, count, count), F32),
            pltpu.VMEM((PLANE, 2, count, width // 4), BF16),
            pltpu.VMEM((PLANE, tile_cols, width // 4), BF16),
            pltpu.VMEM((PLANE, tile_cols, width // 4), BF16),
            pltpu.VMEM((PLANE, heads, count), F32),
            pltpu.VMEM((2, count, heads), F32),
            pltpu.VMEM((2, heads, count), F32),
            pltpu.VMEM((2, count, width), F32),
            pltpu.VMEM((8, width), F32),
            pltpu.VMEM((gp, 8, lanes), F32),
            pltpu.VMEM((depth, gp, 8, lanes), F32),
            pltpu.VMEM((2, pairs, hd, lanes), F32),
            pltpu.VMEM((2, pairs, hd, lanes), F32),
            pltpu.VMEM((3, pairs, 8, lanes), F32),
            pltpu.VMEM((2, gp, hd, lanes), BF16),
            pltpu.VMEM((depth, gp, hd, lanes), BF16),
            pltpu.VMEM((2, pairs, hd, lanes), F32),
            pltpu.VMEM((pairs, count, lanes), F32),
            pltpu.VMEM((PLANE, count, gw), BF16),
            pltpu.VMEM((PLANE, count, gw), BF16),
            pltpu.VMEM((2, count, lanes), F32),
            dma, dma, dma((PIECES,)), dma, dma,
            dma, dma((3,)), dma((2,)), dma((2, depth)), dma((2,)),
            dma((PLANE, 2)), dma((PLANE, 2)),
            dma((2,)), dma((2, PLANE)), dma((2, PLANE)),
            dma, dma, dma, dma, dma, dma, dma, dma,
        ],
        compiler_params=pltpu.CompilerParams(
            collective_id=0, has_side_effects=True, vmem_limit_bytes=60 * 1024 * 1024),
    )(
        x.reshape(count, width), ratios, w, retention,
        credit.reshape(1, width), gain.reshape(1, width),
        scale.reshape(1, 4 * width), offset.reshape(1, 4 * width),
    )


def solution(mesh):
    return jax.shard_map(
        body,
        mesh=mesh,
        in_specs=(
            P("row", "col", None),
            P(),
            P(None, "row", None),
            P(None, "row", "col"),
            P(),
            P(),
            P(),
            P(),
        ),
        out_specs=P("row", "col", None),
        check_vma=False,
    )
```

time: 57.1 us -> 50.2 us (0.88)
  Pallas kernels: 55 us -> 48.1 us
    pallas_call x1, Pallas kernels: 55 us -> 48.1 us  [body(): pl.pallas_call(functools.partial(kernel, rows, cols, tile_rows, tile_cols...]
where the time goes in v2:
time: 50.2 us; the launch traced here: 49.9 us
  Pallas kernels  48.1 us (96%)
  local copies, waits for them, and re-layouts  1.87 us (4%)
    pallas_call x1, Pallas kernels, body(): pl.pallas_call(functools.partial(kernel, rows, cols, tile_rows, tile_cols...  48.1 us
    unnamed x1, local copies, waits for them, and re-layouts  1.87 us

profile of v2, /device:TPU:0, one launch (start us, length us, event | category | flops | bytes accessed | tf_op | source)
XLA Modules:
  0.0 49.9 jit_solution(6777637836126349524)
XLA Ops:
  0.0 48.1 %shard_map.82 = bf16[4,16,4096]{2,1,0:T(8,128)(2,1)} custom-call(bf16[256,1024]{1,0:T(8,128)(2,1)} %bitcast.5, f32[3,1024]{1,0:T(4,128)} %ratio_ref.1, bf16[3,64,1024]{2,1,0:T(8,128)(2,1)} %w_ref.1, f32[16,8,32]{2,1,0:T(8,128)} %ret_ref.1, f32[1,1024]{1,0:T(1,128)} %bitcast.8, f32[1,1024]{1,0:T(1,128)} %bitcast.9, f32[1,4096]{1,0:T(1,128)} %bitcast.6, ...), custom_call_target="tpu_custom_call" | custom-call | tf_op jit(solution)/shard_map/pallas_call | solution.py:526
  48.1 1.9 %copy.10 = bf16[4,16,4096]{2,1,0:T(8,128)(2,1)} copy(bf16[4,16,4096]{2,1,0:T(8,128)(2,1)} %shard_map.82) | data formatting | bytes 1048576

commit v3 on v2

--- a/solution.py
+++ b/solution.py
@@ -27,11 +27,12 @@
 
 def kernel(
     rows, cols, tile_rows, tile_cols, heads,
-    x_ref, ratio_ref, w_ref, ret_ref, credit_ref, gain_ref, scale_ref, offset_ref,
-    out_ref,
-    xt, wf, mx, proj, decay, side, top_rows, bottom_rows, rets, rows_t, rows_r, spread_t, log_t, plane_log, plane_logs,
+    x_ref, ratio_hbm, w_ref, ret_hbm, credit_hbm, gain_hbm, scale_hbm, offset_hbm,
+    out_hbm,
+    ratio_ref, ret_ref, credit_ref, gain_ref, scale_ref, offset_ref, out_ref, shift_t,
+    xt, wf, mx, proj, decay, side, top_rows, bottom_rows, ret_out, rets, rows_t, rows_r, spread_t, log_t, plane_log, plane_logs,
     sums, before, decays_t, plane_sum, plane_sums, entering, block, sent, landed, stats,
-    x_own, x_send, x_piece, x_near, x_far, w_own, w_send, w_plane, w_z, w_mate, side_send, side_recv, edge_own,
+    small_in, out_left, x_own, x_send, x_piece, x_near, x_far, w_own, w_send, w_plane, w_z, w_mate, side_send, side_recv,
     edge_send, edge_recv, ret_send, ret_recv, log_send, log_recv, sum_send, sum_recv, out_send, out_recv,
 ):
     count, width = xt.shape[1:]
@@ -56,10 +57,6 @@
     base = z * PLANE
     first_row, second_row = base + q1, base + q2
     right, left = (col + 1) % cols, (col + cols - 1) % cols
-    sends_down = (q < PLANE - 1) | (z < depth - 1)
-    sends_up = (q > 0) | (z > 0)
-    down_plane = jnp.where(q < PLANE - 1, z, (z + 1) % depth)
-    up_plane = jnp.where(q > 0, z, (z + depth - 1) % depth)
     down_slot, up_slot = (q + 1) % PLANE, (q + PLANE - 1) % PLANE
 
     barrier = pltpu.get_barrier_semaphore()
@@ -100,13 +97,24 @@
     def my_cols(qq):
         return pl.ds(pl.multiple_of(qq * gw, gw), gw)
 
+    small = [
+        local(src, dst, small_in.at[k])
+        for k, (src, dst) in enumerate((
+            (ret_hbm, ret_ref), (ratio_hbm, ratio_ref), (credit_hbm, credit_ref), (gain_hbm, gain_ref),
+            (scale_hbm, scale_ref), (offset_hbm, offset_ref)))
+    ]
+    for c in small:
+        c.start()
     x_copy = local(x_ref, xt.at[q], x_own)
     w_copy = local(w_ref.at[:, my_rows, my_cols(q)], wf.at[:, z, q, half], w_own)
     w_copy.start()
     x_copy.start()
     top_source = x_ref.at[count - tile_cols:count, 2 * quarter:3 * quarter]
     bottom_source = x_ref.at[0:tile_cols, 3 * quarter:]
-    rets[q] = jnp.concatenate([ret_ref[:, r, :] for r in range(tile_rows)], axis=1)
+    small[0].wait()
+    own_ret = jnp.concatenate([ret_ref[:, r, :] for r in range(tile_rows)], axis=1)
+    for qq in range(PLANE):
+        ret_out[qq, 0:hp] = own_ret[qq * hp:(qq + 1) * hp]
 
     expected = (
         depth + PLANE + 1
@@ -130,38 +138,32 @@
         ]
 
     def edges(act):
+        @pl.when(q < PLANE - 1)
+        def _():
+            act(remote(top_source, top_rows.at[down_slot], edge_send.at[0, 0], edge_recv.at[0, down_slot],
+                       {"row": base + q12}))
+
+        @pl.when(q > 0)
+        def _():
+            act(remote(bottom_source, bottom_rows.at[up_slot], edge_send.at[1, 0], edge_recv.at[1, up_slot],
+                       {"row": base + q12}))
+
         for qq in range(PLANE):
-            to = down_plane * PLANE + qq
-
-            @pl.when(sends_down & (to != row))
+            @pl.when((q == PLANE - 1) & (z < depth - 1))
             def _():
                 act(remote(top_source, top_rows.at[down_slot], edge_send.at[0, qq], edge_recv.at[0, down_slot],
-                           {"row": to}))
-
-            to_up = up_plane * PLANE + qq
-
-            @pl.when(sends_up & (to_up != row))
+                           {"row": (base + PLANE + qq) % rows}))
+
+            @pl.when((q == 0) & (z > 0))
             def _():
                 act(remote(bottom_source, bottom_rows.at[up_slot], edge_send.at[1, qq], edge_recv.at[1, up_slot],
-                           {"row": to_up}))
-
-    top_own = local(top_source, top_rows.at[down_slot], edge_own.at[0])
-    bottom_own = local(bottom_source, bottom_rows.at[up_slot], edge_own.at[1])
-
-    def own_edges(act):
-        @pl.when(q < PLANE - 1)
-        def _():
-            act(top_own)
-
-        @pl.when(q > 0)
-        def _():
-            act(bottom_own)
+                           {"row": (base + rows - PLANE + qq) % rows}))
 
     weights_to_plane(KV, 0)
     for o in range(1, PLANE):
-        remote(rets.at[q], rets.at[q], ret_send, ret_recv, {"row": base + (q + o) % PLANE}).start()
+        qq = (q + o) % PLANE
+        remote(ret_out.at[qq], rets.at[q], ret_send, ret_recv, {"row": base + qq}).start()
     edges(lambda c: c.start())
-    own_edges(lambda c: c.start())
     for c in side_copies(q, x_ref):
         c.start()
     for k in range(PIECES):
@@ -194,12 +196,8 @@
     weights_along_z(KV, 0)
 
     arrive(rets.at[0:PLANE - 1], ret_recv)
-    all_rets = jnp.concatenate([rets[t] for t in range(PLANE)], axis=0)
-    picks = (
-        iota((heads, PLANE * heads), 1)
-        == iota((heads, PLANE * heads), 0) // hp * heads + q * hp + iota((heads, PLANE * heads), 0) % hp
-    ).astype(F32)
-    ret = jnp.dot(picks, all_rets, precision=HIGH, preferred_element_type=F32)
+    rets[q] = ret_out[q]
+    ret = jnp.concatenate([rets[t, 0:hp] for t in range(PLANE)], axis=0)
     tri = (iota((count, count), 0) >= iota((count, count), 1)).astype(F32)
     contract_last = (((1,), (1,)), ((), ()))
     running_c = lax.dot_general(tri, ret, contract_last, precision=HIGH, preferred_element_type=F32)
@@ -262,15 +260,21 @@
             c.start()
 
     def edges_in():
-        own_edges(lambda c: c.wait())
-        for t in range(PLANE):
-            @pl.when((base + t > 0) & (q != t - 1))
-            def _():
-                arrive(top_rows.at[t], edge_recv.at[0, t])
-
-            @pl.when((base + t < rows - 1) & (q != t + 1))
-            def _():
-                arrive(bottom_rows.at[t], edge_recv.at[1, t])
+        @pl.when(z > 0)
+        def _():
+            arrive(top_rows.at[0], edge_recv.at[0, 0])
+
+        @pl.when(z < depth - 1)
+        def _():
+            arrive(bottom_rows.at[PLANE - 1], edge_recv.at[1, PLANE - 1])
+
+        @pl.when(q12 < PLANE - 1)
+        def _():
+            arrive(top_rows.at[0], edge_recv.at[0, (q12 + 1) % PLANE])
+
+        @pl.when(q12 > 0)
+        def _():
+            arrive(bottom_rows.at[0], edge_recv.at[1, (q12 + PLANE - 1) % PLANE])
 
     place_in_row = iota((count, quarter), 0) % tile_cols
     last = tile_cols - 1
@@ -282,8 +286,13 @@
         x1 = xt[t, :, quarter:2 * quarter].astype(F32)
         side0 = jnp.where(col > 0, side[t, 0].astype(F32), 0.0)
         side1 = jnp.where(col < cols - 1, side[t, 1].astype(F32), 0.0)
-        top = jnp.where(base + t > 0, top_rows[t].astype(F32), 0.0)
-        bottom = jnp.where(base + t < rows - 1, bottom_rows[t].astype(F32), 0.0)
+        up_t, down_t = (t + PLANE - 1) % PLANE, (t + 1) % PLANE
+        up_sent, down_sent = (t == 0) | (up_t == q12), (t == PLANE - 1) | (down_t == q12)
+        up_t, down_t = jnp.where(up_sent, t, up_t), jnp.where(down_sent, t, down_t)
+        above = xt[up_t, count - tile_cols:count, 2 * quarter:3 * quarter].astype(F32)
+        below = xt[down_t, 0:tile_cols, 3 * quarter:].astype(F32)
+        top = jnp.where(base + t > 0, jnp.where(up_sent, top_rows[t].astype(F32), above), 0.0)
+        bottom = jnp.where(base + t < rows - 1, jnp.where(down_sent, bottom_rows[t].astype(F32), below), 0.0)
         shifted = [
             jnp.where(place_in_row == 0, pltpu.roll(side0, count - last, 0), pltpu.roll(x0, 1, 0)),
             jnp.where(place_in_row == last, pltpu.roll(side1, last, 0), pltpu.roll(x1, count - 1, 0)),
@@ -385,7 +394,7 @@
 
         lax.fori_loop(0, gp, one, 0)
 
-    def finish(t, dst):
+    def finish(t, dst, send=None):
         def one(j, carry):
             vp = t * gp + j
             span = span_of(vp)
@@ -404,36 +413,75 @@
             centred = wkv - halves(wkv) * (1.0 / hd)
             variance = halves(centred * centred) * (1.0 / hd)
             normed = centred * lax.rsqrt(variance + 1e-05) * gain_ref[:, channels(j)]
-            dst[t, :, span_of(j)] = normed.astype(BF16)
+            dst[t, j] = normed.astype(BF16)
+            if send is not None:
+                send(t, j)
             return carry
 
         lax.fori_loop(0, gp, one, 0)
 
     def finish_and_send(t):
-        finish(t, sent)
-        remote(sent.at[t], landed.at[q], out_send, out_recv, {"row": base + t}).start()
+        finish(t, sent, lambda t, j: remote(
+            sent.at[t, j], landed.at[q, j], out_send, out_recv.at[q], {"row": base + t}).start())
+
+    group = (
+        (iota((count, count), 0) // (2 * tile_cols) == iota((count, count), 1) // (2 * tile_cols))
+        & (iota((count, count), 0) % tile_cols // 2 == iota((count, count), 1) % tile_cols // 2)
+    ).astype(BF16)
+
+    def over_group(values):
+        terms = []
+        for value in values:
+            terms.extend(two_terms(jnp.broadcast_to(jnp.sum(value, axis=1, keepdims=True), (count, lanes))))
+        both = jnp.dot(group, jnp.concatenate(terms, axis=1), preferred_element_type=F32) * (1.0 / (4 * width))
+        return [
+            both[:, 2 * k * lanes:(2 * k + 1) * lanes] + both[:, (2 * k + 1) * lanes:(2 * k + 2) * lanes]
+            for k in range(len(values))
+        ]
+
+    none = jnp.zeros((count, lanes), F32)
+
+    def mean_of_x():
+        total = none
+        for i in range(vp_count):
+            total = total + xt[q, :, i * lanes:(i + 1) * lanes].astype(F32)
+        shift_t[...] = over_group([total])[0]
+
+    def add_up(t, carry):
+        def one(j, carry):
+            first, second = carry
+            i = t * gp + j
+            made = xt[q, :, span_of(i)].astype(F32) - shift_t[...] + landed[t, j].astype(F32)
+            block[i] = made
+            return first + made, second + made * made
+
+        return lax.fori_loop(0, gp, one, carry)
+
+    for c in small[1:]:
+        c.wait()
 
     some_decays(0)
     x_copy.wait()
+    mean_of_x()
     edges_in()
+    some_decays(1)
     forward(0)
-    mix(q)
     forward(1)
-    some_decays(1)
+    some_decays(2)
     forward(2)
-    some_decays(2)
-    weights_from_z(KV, 0)
+    some_decays(3)
     forward(3)
     sides_out(q1)
-    weights_along_z(R, 1)
-    some_decays(3)
     arrive(xt.at[q2], x_near)
     sides_out(q2)
+    weights_from_z(KV, 0)
+    weights_along_z(R, 1)
+    mix(q)
+    mix(q1)
+    mix(q2)
     weights_from_mate(KV, 0)
     keys_values(q)
-    mix(q1)
     keys_values(q1)
-    mix(q2)
     keys_values(q2)
     arrive(xt.at[q12], x_far)
     sides_out(q12)
@@ -455,46 +503,28 @@
     project(0, q)
     local_mix(q)
     finish(q, landed)
-    arrive(landed.at[0:PLANE - 1], out_recv)
-
-    group = (
-        (iota((count, count), 0) // (2 * tile_cols) == iota((count, count), 1) // (2 * tile_cols))
-        & (iota((count, count), 0) % tile_cols // 2 == iota((count, count), 1) % tile_cols // 2)
-    ).astype(BF16)
-
-    def over_group(value):
-        rowsum = jnp.broadcast_to(jnp.sum(value, axis=1, keepdims=True), (count, lanes))
-        both = jnp.dot(group, jnp.concatenate(two_terms(rowsum), axis=1), preferred_element_type=F32)
-        return (both[:, 0:lanes] + both[:, lanes:]) * (1.0 / (4 * width))
-
-    def add_up(i, total):
-        made = xt[q, :, span_of(i)].astype(F32) + landed[i // gp, :, span_of(i % gp)].astype(F32)
-        block[i] = made
-        return total + made
-
-    none = jnp.zeros((count, lanes), F32)
-    mean = over_group(lax.fori_loop(0, vp_count, add_up, none))
-
-    def spread(i, acc):
-        dev = block[i] - mean
-        return acc + dev * dev
-
-    variance = over_group(lax.fori_loop(0, vp_count, spread, none))
+    carry = add_up(q, (none, none))
+    for t in (q1, q2, q12):
+        arrive(landed.at[t], out_recv.at[t])
+        carry = add_up(t, carry)
+
+    mean, square = over_group(carry)
     stats[0] = mean
-    stats[1] = lax.rsqrt(variance + 1e-05)
+    stats[1] = lax.rsqrt(jnp.maximum(square - mean * mean, 0.0) + 1e-05)
     half_cols = tile_cols // 2
-
-    def emit(i, carry):
-        for part in range(4):
-            span = pl.ds(pl.multiple_of(part * width + i * lanes, lanes), lanes)
-            g, o = scale_ref[:, span], offset_ref[:, span]
-            for a in range(tile_rows // 2):
+    outs = []
+    for a in range(tile_rows // 2):
+        def emit(i, carry):
+            for part in range(4):
+                span = pl.ds(pl.multiple_of(part * width + i * lanes, lanes), lanes)
                 take = pl.ds((2 * a + part % 2) * tile_cols + part // 2, half_cols, stride=2)
                 value = (block[i, take, :] - stats[0, take, :]) * stats[1, take, :]
-                out_ref[a, :, span] = (value * g + o).astype(BF16)
-        return carry
-
-    lax.fori_loop(0, vp_count, emit, 0)
+                out_ref[a, :, span] = (value * scale_ref[:, span] + offset_ref[:, span]).astype(BF16)
+            return carry
+
+        lax.fori_loop(0, vp_count, emit, 0)
+        outs.append(local(out_ref.at[a], out_hbm.at[a], out_left.at[a]))
+        outs[-1].start()
 
     left_by(xt.at[0:3], x_send)
     left_by(wf.at[:, z, 0:PLANE - 1, half], w_send.at[0])
@@ -508,6 +538,8 @@
     for t in range(PLANE):
         for c in side_copies(t, xt.at[t]):
             c.wait_send()
+    for c in outs:
+        c.wait()
 
 
 def body(x, ratios, w, retention, credit, gain, scale, offset):
@@ -522,13 +554,21 @@
     gw = width // PLANE
     gp = gw // lanes
     dma = pltpu.SemaphoreType.DMA
-    anywhere, vmem = pl.BlockSpec(memory_space=pl.ANY), pl.BlockSpec(memory_space=pltpu.VMEM)
+    anywhere = pl.BlockSpec(memory_space=pl.ANY)
     return pl.pallas_call(
         functools.partial(kernel, rows, cols, tile_rows, tile_cols, heads),
         out_shape=jax.ShapeDtypeStruct((tile_rows // 2, tile_cols // 2, 4 * width), BF16),
-        in_specs=[anywhere, vmem, anywhere, vmem, vmem, vmem, vmem, vmem],
-        out_specs=vmem,
+        in_specs=[anywhere] * 8,
+        out_specs=anywhere,
         scratch_shapes=[
+            pltpu.VMEM((3, width), F32),
+            pltpu.VMEM((heads, tile_rows, tile_cols), F32),
+            pltpu.VMEM((1, width), F32),
+            pltpu.VMEM((1, width), F32),
+            pltpu.VMEM((1, 4 * width), F32),
+            pltpu.VMEM((1, 4 * width), F32),
+            pltpu.VMEM((tile_rows // 2, tile_cols // 2, 4 * width), BF16),
+            pltpu.VMEM((count, lanes), F32),
             pltpu.VMEM((PLANE, count, width), BF16),
             pltpu.VMEM((3, depth, PLANE, 2, w.shape[1] // 2, gw), BF16),
             pltpu.VMEM((PLANE, 3, count, width), BF16),
@@ -537,7 +577,8 @@
             pltpu.VMEM((PLANE, 2, count, width // 4), BF16),
             pltpu.VMEM((PLANE, tile_cols, width // 4), BF16),
             pltpu.VMEM((PLANE, tile_cols, width // 4), BF16),
-            pltpu.VMEM((PLANE, heads, count), F32),
+            pltpu.VMEM((PLANE, 8, count), F32),
+            pltpu.VMEM((PLANE, 8, count), F32),
             pltpu.VMEM((2, count, heads), F32),
             pltpu.VMEM((2, heads, count), F32),
             pltpu.VMEM((2, count, width), F32),
@@ -551,14 +592,15 @@
             pltpu.VMEM((depth, gp, hd, lanes), BF16),
             pltpu.VMEM((2, pairs, hd, lanes), F32),
             pltpu.VMEM((pairs, count, lanes), F32),
-            pltpu.VMEM((PLANE, count, gw), BF16),
-            pltpu.VMEM((PLANE, count, gw), BF16),
+            pltpu.VMEM((PLANE, gp, count, lanes), BF16),
+            pltpu.VMEM((PLANE, gp, count, lanes), BF16),
             pltpu.VMEM((2, count, lanes), F32),
+            dma((6,)), dma((tile_rows // 2,)),
             dma, dma, dma((PIECES,)), dma, dma,
             dma, dma((3,)), dma((2,)), dma((2, depth)), dma((2,)),
             dma((PLANE, 2)), dma((PLANE, 2)),
-            dma((2,)), dma((2, PLANE)), dma((2, PLANE)),
-            dma, dma, dma, dma, dma, dma, dma, dma,
+            dma((2, PLANE)), dma((2, PLANE)),
+            dma, dma, dma, dma, dma, dma, dma, dma((PLANE,)),
         ],
         compiler_params=pltpu.CompilerParams(
             collective_id=0, has_side_effects=True, vmem_limit_bytes=60 * 1024 * 1024),

time: 50.2 us -> 47.9 us (0.954)
  Pallas kernels: 48.1 us -> 45.9 us
    pallas_call x1, Pallas kernels: 48.1 us -> 45.9 us  [body(): pl.pallas_call(functools.partial(kernel, rows, cols, tile_rows, tile_cols...]
where the time goes in v3:
time: 47.9 us; the launch traced here: 47.7 us
  Pallas kernels  45.9 us (96%)
  local copies, waits for them, and re-layouts  1.87 us (4%)
    pallas_call x1, Pallas kernels, body(): pl.pallas_call(functools.partial(kernel, rows, cols, tile_rows, tile_cols...  45.9 us
    unnamed x1, local copies, waits for them, and re-layouts  1.87 us

profile of v3, /device:TPU:0, one launch (start us, length us, event | category | flops | bytes accessed | tf_op | source)
XLA Modules:
  0.0 47.7 jit_solution(5789249576668199325)
XLA Ops:
  0.0 45.9 %shard_map.82 = bf16[4,16,4096]{2,1,0:T(8,128)(2,1)} custom-call(bf16[256,1024]{1,0:T(8,128)(2,1)} %bitcast.5, f32[3,1024]{1,0:T(4,128)} %ratio_hbm.1, bf16[3,64,1024]{2,1,0:T(8,128)(2,1)} %w_ref.1, f32[16,8,32]{2,1,0:T(8,128)} %ret_hbm.1, f32[1,1024]{1,0:T(1,128)} %bitcast.8, f32[1,1024]{1,0:T(1,128)} %bitcast.9, f32[1,4096]{1,0:T(1,128)} %bitcast.6, ...), custom_call_target="tpu_custom_call" | custom-call | tf_op jit(solution)/shard_map/pallas_call | solution.py:558
  45.9 1.9 %copy.10 = bf16[4,16,4096]{2,1,0:T(8,128)(2,1)} copy(bf16[4,16,4096]{2,1,0:T(8,128)(2,1)} %shard_map.82) | data formatting | bytes 1048576

commit v4 on v3

--- a/solution.py
+++ b/solution.py
@@ -30,9 +30,9 @@
     x_ref, ratio_hbm, w_ref, ret_hbm, credit_hbm, gain_hbm, scale_hbm, offset_hbm,
     out_hbm,
     ratio_ref, ret_ref, credit_ref, gain_ref, scale_ref, offset_ref, out_ref, shift_t,
-    xt, wf, mx, proj, decay, side, top_rows, bottom_rows, ret_out, rets, rows_t, rows_r, spread_t, log_t, plane_log, plane_logs,
+    xt, wf, mx, proj, decay, side, side_out, side_far, top_rows, bottom_rows, ret_out, rets, rows_t, rows_r, spread_t, log_t, plane_log, plane_logs,
     sums, before, decays_t, plane_sum, plane_sums, entering, block, sent, landed, stats,
-    small_in, out_left, x_own, x_send, x_piece, x_near, x_far, w_own, w_send, w_plane, w_z, w_mate, side_send, side_recv,
+    small_in, out_left, x_own, x_send, x_piece, x_near, x_far, w_own, w_send, w_plane, w_z, w_mate, side_send, side_recv, far_send, far_recv,
     edge_send, edge_recv, ret_send, ret_recv, log_send, log_recv, sum_send, sum_recv, out_send, out_recv,
 ):
     count, width = xt.shape[1:]
@@ -279,13 +279,34 @@
     place_in_row = iota((count, quarter), 0) % tile_cols
     last = tile_cols - 1
 
-    def mix(t):
-        for c in side_copies(t, xt.at[t]):
+    def far_sides_out():
+        for c in side_copies(q, x_ref):
             c.wait_recv()
+        token, line = iota((tile_rows, count), 1), iota((tile_rows, count), 0) * tile_cols
+        for k in range(2):
+            pick = (token == line + (last if k == 0 else 0)).astype(BF16)
+            side_out[k] = jnp.dot(pick, side[q, k], preferred_element_type=F32).astype(BF16)
+        remote(side_out, side_far, far_send, far_recv, {"row": base + q12}).start()
+
+    def mix(t, kind):
         x0 = xt[t, :, 0:quarter].astype(F32)
         x1 = xt[t, :, quarter:2 * quarter].astype(F32)
-        side0 = jnp.where(col > 0, side[t, 0].astype(F32), 0.0)
-        side1 = jnp.where(col < cols - 1, side[t, 1].astype(F32), 0.0)
+        if kind == "far":
+            arrive(side_far, far_recv)
+            token, line = iota((count, tile_rows), 0), iota((count, tile_rows), 1) * tile_cols
+            side0, side1 = [
+                jnp.dot((token == line + (0 if k == 0 else last)).astype(BF16), side_far[k],
+                        preferred_element_type=F32)
+                for k in range(2)
+            ]
+        else:
+            if kind == "near":
+                for c in side_copies(t, xt.at[t]):
+                    c.wait_recv()
+            side0 = pltpu.roll(side[t, 0].astype(F32), count - last, 0)
+            side1 = pltpu.roll(side[t, 1].astype(F32), last, 0)
+        side0 = jnp.where(col > 0, side0, 0.0)
+        side1 = jnp.where(col < cols - 1, side1, 0.0)
         up_t, down_t = (t + PLANE - 1) % PLANE, (t + 1) % PLANE
         up_sent, down_sent = (t == 0) | (up_t == q12), (t == PLANE - 1) | (down_t == q12)
         up_t, down_t = jnp.where(up_sent, t, up_t), jnp.where(down_sent, t, down_t)
@@ -294,8 +315,8 @@
         top = jnp.where(base + t > 0, jnp.where(up_sent, top_rows[t].astype(F32), above), 0.0)
         bottom = jnp.where(base + t < rows - 1, jnp.where(down_sent, bottom_rows[t].astype(F32), below), 0.0)
         shifted = [
-            jnp.where(place_in_row == 0, pltpu.roll(side0, count - last, 0), pltpu.roll(x0, 1, 0)),
-            jnp.where(place_in_row == last, pltpu.roll(side1, last, 0), pltpu.roll(x1, count - 1, 0)),
+            jnp.where(place_in_row == 0, side0, pltpu.roll(x0, 1, 0)),
+            jnp.where(place_in_row == last, side1, pltpu.roll(x1, count - 1, 0)),
             jnp.concatenate([top, xt[t, 0:count - tile_cols, 2 * quarter:3 * quarter].astype(F32)], axis=0),
             jnp.concatenate([xt[t, tile_cols:count, 3 * quarter:].astype(F32), bottom], axis=0),
         ]
@@ -460,6 +481,7 @@
     for c in small[1:]:
         c.wait()
 
+    far_sides_out()
     some_decays(0)
     x_copy.wait()
     mean_of_x()
@@ -476,19 +498,18 @@
     sides_out(q2)
     weights_from_z(KV, 0)
     weights_along_z(R, 1)
-    mix(q)
-    mix(q1)
-    mix(q2)
+    mix(q, "own")
+    mix(q1, "near")
+    mix(q2, "near")
     weights_from_mate(KV, 0)
     keys_values(q)
     keys_values(q1)
     keys_values(q2)
     arrive(xt.at[q12], x_far)
-    sides_out(q12)
-    weights_from_z(R, 1)
-    mix(q12)
+    mix(q12, "far")
     keys_values(q12)
     planes_out()
+    weights_from_z(R, 1)
     weights_from_mate(R, 1)
     project(0, q1)
     local_mix(q1)
@@ -535,9 +556,10 @@
     left_by(plane_sums.at[0:depth - 1], sum_send)
     left_by(sent.at[0:PLANE - 1], out_send)
     edges(lambda c: c.wait_send())
-    for t in range(PLANE):
+    for t in (q, q1, q2):
         for c in side_copies(t, xt.at[t]):
             c.wait_send()
+    left_by(side_out, far_send)
     for c in outs:
         c.wait()
 
@@ -575,6 +597,8 @@
             pltpu.VMEM((3, count, width), BF16),
             pltpu.VMEM((heads, count, count), F32),
             pltpu.VMEM((PLANE, 2, count, width // 4), BF16),
+            pltpu.VMEM((2, tile_rows, width // 4), BF16),
+            pltpu.VMEM((2, tile_rows, width // 4), BF16),
             pltpu.VMEM((PLANE, tile_cols, width // 4), BF16),
             pltpu.VMEM((PLANE, tile_cols, width // 4), BF16),
             pltpu.VMEM((PLANE, 8, count), F32),
@@ -598,17 +622,19 @@
             dma((6,)), dma((tile_rows // 2,)),
             dma, dma, dma((PIECES,)), dma, dma,
             dma, dma((3,)), dma((2,)), dma((2, depth)), dma((2,)),
-            dma((PLANE, 2)), dma((PLANE, 2)),
+            dma((PLANE, 2)), dma((PLANE, 2)), dma, dma,
             dma((2, PLANE)), dma((2, PLANE)),
             dma, dma, dma, dma, dma, dma, dma, dma((PLANE,)),
         ],
         compiler_params=pltpu.CompilerParams(
-            collective_id=0, has_side_effects=True, vmem_limit_bytes=60 * 1024 * 1024),
-    )(
-        x.reshape(count, width), ratios, w, retention,
-        credit.reshape(1, width), gain.reshape(1, width),
-        scale.reshape(1, 4 * width), offset.reshape(1, 4 * width),
-    )
+            collective_id=0, has_side_effects=True, vmem_limit_bytes=40 * 1024 * 1024),
+    )(*[
+        pltpu.with_memory_space_constraint(value, pltpu.MemorySpace.HBM)
+        for value in (
+            x.reshape(count, width), ratios, w, retention,
+            credit.reshape(1, width), gain.reshape(1, width),
+            scale.reshape(1, 4 * width), offset.reshape(1, 4 * width))
+    ])
 
 
 def solution(mesh):

time: 47.9 us -> 45.8 us (0.956)
  local copies, waits for them, and re-layouts: 1.87 us -> 0.8 us
  Pallas kernels: 45.9 us -> 44.9 us
    unnamed x1, local copies, waits for them, and re-layouts: 1.87 us -> 0.8 us
    pallas_call x1, Pallas kernels: 45.9 us -> 44.9 us  [body(): pl.pallas_call(functools.partial(kernel, rows, cols, tile_rows, tile_cols...]
where the time goes in v4:
time: 45.8 us; the launch traced here: 45.7 us
  Pallas kernels  44.9 us (98%)
  local copies, waits for them, and re-layouts  0.8 us (2%)
    pallas_call x1, Pallas kernels, body(): pl.pallas_call(functools.partial(kernel, rows, cols, tile_rows, tile_cols...  44.9 us

profile of v4, /device:TPU:0, one launch (start us, length us, event | category | flops | bytes accessed | tf_op | source)
XLA Modules:
  0.0 45.7 jit_solution(15491918945188777045)
XLA Ops:
  0.0 44.9 %shard_map.82 = bf16[4,16,4096]{2,1,0:T(8,128)(2,1)S(1)} custom-call(bf16[256,1024]{1,0:T(8,128)(2,1)} %bitcast.5, f32[3,1024]{1,0:T(4,128)} %ratio_hbm.1, bf16[3,64,1024]{2,1,0:T(8,128)(2,1)} %w_ref.1, f32[16,8,32]{2,1,0:T(8,128)} %ret_hbm.1, f32[1,1024]{1,0:T(1,128)} %bitcast.8, f32[1,1024]{1,0:T(1,128)} %bitcast.9, f32[1,4096]{1,0:T(1,128)} %bitcast.6, ...), custom_call_target="tpu_custom_call" | custom-call | tf_op jit(solution)/shard_map/pallas_call | solution.py:580
  44.9 0.8 %copy.10 = bf16[4,16,4096]{2,1,0:T(8,128)(2,1)} copy(bf16[4,16,4096]{2,1,0:T(8,128)(2,1)S(1)} %shard_map.82) | data formatting | bytes 1048576

commit v5 on v4

--- a/solution.py
+++ b/solution.py
@@ -169,7 +169,6 @@
     for k in range(PIECES):
         part = slice(k * piece, (k + 1) * piece)
         remote(x_ref.at[part], xt.at[q, part], x_send, x_piece.at[k], {"row": first_row}).start()
-    remote(x_ref, xt.at[q], x_send, x_near, {"row": second_row}).start()
     weights_to_plane(R, 1)
 
     def weights_to_mate(which, k, zz):
@@ -196,6 +195,7 @@
     weights_along_z(KV, 0)
 
     arrive(rets.at[0:PLANE - 1], ret_recv)
+    remote(x_ref, xt.at[q], x_send, x_near, {"row": second_row}).start()
     rets[q] = ret_out[q]
     ret = jnp.concatenate([rets[t, 0:hp] for t in range(PLANE)], axis=0)
     tri = (iota((count, count), 0) >= iota((count, count), 1)).astype(F32)
@@ -353,7 +353,7 @@
             sums[1, vp] = jnp.where(low_u, m[2 * hd:3 * hd], m[3 * hd:])
             return carry
 
-        lax.fori_loop(0, gp, one, 0)
+        lax.fori_loop(0, gp, one, 0, unroll=True)
 
     def keys_values(t):
         project(1, t)
@@ -439,7 +439,7 @@
                 send(t, j)
             return carry
 
-        lax.fori_loop(0, gp, one, 0)
+        lax.fori_loop(0, gp, one, 0, unroll=True)
 
     def finish_and_send(t):
         finish(t, sent, lambda t, j: remote(
@@ -476,7 +476,7 @@
             block[i] = made
             return first + made, second + made * made
 
-        return lax.fori_loop(0, gp, one, carry)
+        return lax.fori_loop(0, gp, one, carry, unroll=True)
 
     for c in small[1:]:
         c.wait()
@@ -543,7 +543,7 @@
                 out_ref[a, :, span] = (value * scale_ref[:, span] + offset_ref[:, span]).astype(BF16)
             return carry
 
-        lax.fori_loop(0, vp_count, emit, 0)
+        lax.fori_loop(0, vp_count, emit, 0, unroll=4)
         outs.append(local(out_ref.at[a], out_hbm.at[a], out_left.at[a]))
         outs[-1].start()
 

time: 45.8 us -> 45.1 us (0.985)
  Pallas kernels: 44.9 us -> 44.1 us
    pallas_call x1, Pallas kernels: 44.9 us -> 44.1 us  [body(): pl.pallas_call(functools.partial(kernel, rows, cols, tile_rows, tile_cols...]
where the time goes in v5:
time: 45.1 us; the launch traced here: 45 us
  Pallas kernels  44.1 us (98%)
  local copies, waits for them, and re-layouts  0.8 us (2%)
    pallas_call x1, Pallas kernels, body(): pl.pallas_call(functools.partial(kernel, rows, cols, tile_rows, tile_cols...  44.1 us

profile of v5, /device:TPU:0, one launch (start us, length us, event | category | flops | bytes accessed | tf_op | source)
XLA Modules:
  0.0 45.0 jit_solution(7445704281985468417)
XLA Ops:
  0.0 44.1 %shard_map.82 = bf16[4,16,4096]{2,1,0:T(8,128)(2,1)S(1)} custom-call(bf16[256,1024]{1,0:T(8,128)(2,1)} %bitcast.5, f32[3,1024]{1,0:T(4,128)} %ratio_hbm.1, bf16[3,64,1024]{2,1,0:T(8,128)(2,1)} %w_ref.1, f32[16,8,32]{2,1,0:T(8,128)} %ret_hbm.1, f32[1,1024]{1,0:T(1,128)} %bitcast.8, f32[1,1024]{1,0:T(1,128)} %bitcast.9, f32[1,4096]{1,0:T(1,128)} %bitcast.6, ...), custom_call_target="tpu_custom_call" | custom-call | tf_op jit(solution)/shard_map/pallas_call | solution.py:580
  44.2 0.8 %copy.10 = bf16[4,16,4096]{2,1,0:T(8,128)(2,1)} copy(bf16[4,16,4096]{2,1,0:T(8,128)(2,1)S(1)} %shard_map.82) | data formatting | bytes 1048576

commit v6 on v5

--- a/solution.py
+++ b/solution.py
@@ -28,11 +28,11 @@
 def kernel(
     rows, cols, tile_rows, tile_cols, heads,
     x_ref, ratio_hbm, w_ref, ret_hbm, credit_hbm, gain_hbm, scale_hbm, offset_hbm,
-    out_hbm,
-    ratio_ref, ret_ref, credit_ref, gain_ref, scale_ref, offset_ref, out_ref, shift_t,
+    out_ref,
+    ratio_ref, ret_ref, credit_ref, gain_ref, scale_ref, offset_ref, shift_t,
     xt, wf, mx, proj, decay, side, side_out, side_far, top_rows, bottom_rows, ret_out, rets, rows_t, rows_r, spread_t, log_t, plane_log, plane_logs,
     sums, before, decays_t, plane_sum, plane_sums, entering, block, sent, landed, stats,
-    small_in, out_left, x_own, x_send, x_piece, x_near, x_far, w_own, w_send, w_plane, w_z, w_mate, side_send, side_recv, far_send, far_recv,
+    small_in, x_own, x_send, x_piece, x_near, x_far, w_own, w_send, w_plane, w_z, w_mate, side_send, side_recv, far_send, far_recv,
     edge_send, edge_recv, ret_send, ret_recv, log_send, log_recv, sum_send, sum_recv, out_send, out_recv,
 ):
     count, width = xt.shape[1:]
@@ -544,8 +544,6 @@
             return carry
 
         lax.fori_loop(0, vp_count, emit, 0, unroll=4)
-        outs.append(local(out_ref.at[a], out_hbm.at[a], out_left.at[a]))
-        outs[-1].start()
 
     left_by(xt.at[0:3], x_send)
     left_by(wf.at[:, z, 0:PLANE - 1, half], w_send.at[0])
@@ -581,7 +579,7 @@
         functools.partial(kernel, rows, cols, tile_rows, tile_cols, heads),
         out_shape=jax.ShapeDtypeStruct((tile_rows // 2, tile_cols // 2, 4 * width), BF16),
         in_specs=[anywhere] * 8,
-        out_specs=anywhere,
+        out_specs=pl.BlockSpec(memory_space=pltpu.VMEM),
         scratch_shapes=[
             pltpu.VMEM((3, width), F32),
             pltpu.VMEM((heads, tile_rows, tile_cols), F32),
@@ -589,7 +587,6 @@
             pltpu.VMEM((1, width), F32),
             pltpu.VMEM((1, 4 * width), F32),
             pltpu.VMEM((1, 4 * width), F32),
-            pltpu.VMEM((tile_rows // 2, tile_cols // 2, 4 * width), BF16),
             pltpu.VMEM((count, lanes), F32),
             pltpu.VMEM((PLANE, count, width), BF16),
             pltpu.VMEM((3, depth, PLANE, 2, w.shape[1] // 2, gw), BF16),
@@ -619,7 +616,7 @@
             pltpu.VMEM((PLANE, gp, count, lanes), BF16),
             pltpu.VMEM((PLANE, gp, count, lanes), BF16),
             pltpu.VMEM((2, count, lanes), F32),
-            dma((6,)), dma((tile_rows // 2,)),
+            dma((6,)),
             dma, dma, dma((PIECES,)), dma, dma,
             dma, dma((3,)), dma((2,)), dma((2, depth)), dma((2,)),
             dma((PLANE, 2)), dma((PLANE, 2)), dma, dma,

time: 45.1 us -> 44.3 us (0.982)
  Pallas kernels: 44.1 us -> 43.3 us
    pallas_call x1, Pallas kernels: 44.1 us -> 43.3 us  [body(): pl.pallas_call(functools.partial(kernel, rows, cols, tile_rows, tile_cols...]
where the time goes in v6:
time: 44.3 us; the launch traced here: 44.1 us
  Pallas kernels  43.3 us (98%)
  local copies, waits for them, and re-layouts  0.8 us (2%)
    pallas_call x1, Pallas kernels, body(): pl.pallas_call(functools.partial(kernel, rows, cols, tile_rows, tile_cols...  43.3 us

profile of v6, /device:TPU:0, one launch (start us, length us, event | category | flops | bytes accessed | tf_op | source)
XLA Modules:
  0.0 44.1 jit_solution(15577767611819354911)
XLA Ops:
  0.0 43.3 %shard_map.82 = bf16[4,16,4096]{2,1,0:T(8,128)(2,1)S(1)} custom-call(bf16[256,1024]{1,0:T(8,128)(2,1)} %bitcast.5, f32[3,1024]{1,0:T(4,128)} %ratio_hbm.1, bf16[3,64,1024]{2,1,0:T(8,128)(2,1)} %w_ref.1, f32[16,8,32]{2,1,0:T(8,128)} %ret_hbm.1, f32[1,1024]{1,0:T(1,128)} %bitcast.8, f32[1,1024]{1,0:T(1,128)} %bitcast.9, f32[1,4096]{1,0:T(1,128)} %bitcast.6, ...), custom_call_target="tpu_custom_call" | custom-call | tf_op jit(solution)/shard_map/pallas_call | solution.py:578
  43.3 0.8 %copy.10 = bf16[4,16,4096]{2,1,0:T(8,128)(2,1)} copy(bf16[4,16,4096]{2,1,0:T(8,128)(2,1)S(1)} %shard_map.82) | data formatting | bytes 1048576

commit v7 on v6

--- a/solution.py
+++ b/solution.py
@@ -27,9 +27,9 @@
 
 def kernel(
     rows, cols, tile_rows, tile_cols, heads,
-    x_ref, ratio_hbm, w_ref, ret_hbm, credit_hbm, gain_hbm, scale_hbm, offset_hbm,
+    x_ref, ratio_hbm, w_hbm, ret_hbm, credit_hbm, gain_hbm, scale_hbm, offset_hbm,
     out_ref,
-    ratio_ref, ret_ref, credit_ref, gain_ref, scale_ref, offset_ref, shift_t,
+    ratio_ref, ret_ref, credit_ref, gain_ref, scale_ref, offset_ref, w_ref, shift_t,
     xt, wf, mx, proj, decay, side, side_out, side_far, top_rows, bottom_rows, ret_out, rets, rows_t, rows_r, spread_t, log_t, plane_log, plane_logs,
     sums, before, decays_t, plane_sum, plane_sums, entering, block, sent, landed, stats,
     small_in, x_own, x_send, x_piece, x_near, x_far, w_own, w_send, w_plane, w_z, w_mate, side_send, side_recv, far_send, far_recv,
@@ -101,13 +101,12 @@
         local(src, dst, small_in.at[k])
         for k, (src, dst) in enumerate((
             (ret_hbm, ret_ref), (ratio_hbm, ratio_ref), (credit_hbm, credit_ref), (gain_hbm, gain_ref),
-            (scale_hbm, scale_ref), (offset_hbm, offset_ref)))
+            (scale_hbm, scale_ref), (offset_hbm, offset_ref), (w_hbm, w_ref)))
     ]
     for c in small:
         c.start()
     x_copy = local(x_ref, xt.at[q], x_own)
     w_copy = local(w_ref.at[:, my_rows, my_cols(q)], wf.at[:, z, q, half], w_own)
-    w_copy.start()
     x_copy.start()
     top_source = x_ref.at[count - tile_cols:count, 2 * quarter:3 * quarter]
     bottom_source = x_ref.at[0:tile_cols, 3 * quarter:]
@@ -122,6 +121,10 @@
         + PLANE * ((q == 0) & (z > 0)).astype(jnp.int32)
     )
     pl.semaphore_wait(barrier, expected)
+
+    x_copy.wait()
+    small[6].wait()
+    w_copy.start()
 
     def weights_to_plane(which, k):
         for o in range(1, PLANE):
@@ -168,7 +171,7 @@
         c.start()
     for k in range(PIECES):
         part = slice(k * piece, (k + 1) * piece)
-        remote(x_ref.at[part], xt.at[q, part], x_send, x_piece.at[k], {"row": first_row}).start()
+        remote(xt.at[q, part], xt.at[q, part], x_send, x_piece.at[k], {"row": first_row}).start()
     weights_to_plane(R, 1)
 
     def weights_to_mate(which, k, zz):
@@ -195,7 +198,7 @@
     weights_along_z(KV, 0)
 
     arrive(rets.at[0:PLANE - 1], ret_recv)
-    remote(x_ref, xt.at[q], x_send, x_near, {"row": second_row}).start()
+    remote(xt.at[q], xt.at[q], x_send, x_near, {"row": second_row}).start()
     rets[q] = ret_out[q]
     ret = jnp.concatenate([rets[t, 0:hp] for t in range(PLANE)], axis=0)
     tri = (iota((count, count), 0) >= iota((count, count), 1)).astype(F32)
@@ -478,12 +481,11 @@
 
         return lax.fori_loop(0, gp, one, carry, unroll=True)
 
-    for c in small[1:]:
+    for c in small[1:6]:
         c.wait()
 
     far_sides_out()
     some_decays(0)
-    x_copy.wait()
     mean_of_x()
     edges_in()
     some_decays(1)
@@ -525,26 +527,6 @@
     local_mix(q)
     finish(q, landed)
     carry = add_up(q, (none, none))
-    for t in (q1, q2, q12):
-        arrive(landed.at[t], out_recv.at[t])
-        carry = add_up(t, carry)
-
-    mean, square = over_group(carry)
-    stats[0] = mean
-    stats[1] = lax.rsqrt(jnp.maximum(square - mean * mean, 0.0) + 1e-05)
-    half_cols = tile_cols // 2
-    outs = []
-    for a in range(tile_rows // 2):
-        def emit(i, carry):
-            for part in range(4):
-                span = pl.ds(pl.multiple_of(part * width + i * lanes, lanes), lanes)
-                take = pl.ds((2 * a + part % 2) * tile_cols + part // 2, half_cols, stride=2)
-                value = (block[i, take, :] - stats[0, take, :]) * stats[1, take, :]
-                out_ref[a, :, span] = (value * scale_ref[:, span] + offset_ref[:, span]).astype(BF16)
-            return carry
-
-        lax.fori_loop(0, vp_count, emit, 0, unroll=4)
-
     left_by(xt.at[0:3], x_send)
     left_by(wf.at[:, z, 0:PLANE - 1, half], w_send.at[0])
     left_by(wf.at[:, 0:depth - 1, :, half], w_send.at[1])
@@ -552,14 +534,32 @@
     left_by(rets.at[0:PLANE - 1], ret_send)
     left_by(plane_logs.at[0:depth - 1], log_send)
     left_by(plane_sums.at[0:depth - 1], sum_send)
-    left_by(sent.at[0:PLANE - 1], out_send)
     edges(lambda c: c.wait_send())
     for t in (q, q1, q2):
         for c in side_copies(t, xt.at[t]):
             c.wait_send()
     left_by(side_out, far_send)
-    for c in outs:
-        c.wait()
+    for t in (q1, q2, q12):
+        arrive(landed.at[t], out_recv.at[t])
+        carry = add_up(t, carry)
+
+    mean, square = over_group(carry)
+    stats[0] = mean
+    stats[1] = lax.rsqrt(jnp.maximum(square - mean * mean, 0.0) + 1e-05)
+    half_cols = tile_cols // 2
+    def emit(i, carry):
+        for part in range(4):
+            span = pl.ds(pl.multiple_of(part * width + i * lanes, lanes), lanes)
+            gain, offset = scale_ref[:, span], offset_ref[:, span]
+            for a in range(tile_rows // 2):
+                take = pl.ds((2 * a + part % 2) * tile_cols + part // 2, half_cols, stride=2)
+                value = (block[i, take, :] - stats[0, take, :]) * stats[1, take, :]
+                out_ref[a, :, span] = (value * gain + offset).astype(BF16)
+        return carry
+
+    lax.fori_loop(0, vp_count, emit, 0)
+
+    left_by(sent.at[0:PLANE - 1], out_send)
 
 
 def body(x, ratios, w, retention, credit, gain, scale, offset):
@@ -587,6 +587,7 @@
             pltpu.VMEM((1, width), F32),
             pltpu.VMEM((1, 4 * width), F32),
             pltpu.VMEM((1, 4 * width), F32),
+            pltpu.VMEM(w.shape, BF16),
             pltpu.VMEM((count, lanes), F32),
             pltpu.VMEM((PLANE, count, width), BF16),
             pltpu.VMEM((3, depth, PLANE, 2, w.shape[1] // 2, gw), BF16),
@@ -616,7 +617,7 @@
             pltpu.VMEM((PLANE, gp, count, lanes), BF16),
             pltpu.VMEM((PLANE, gp, count, lanes), BF16),
             pltpu.VMEM((2, count, lanes), F32),
-            dma((6,)),
+            dma((7,)),
             dma, dma, dma((PIECES,)), dma, dma,
             dma, dma((3,)), dma((2,)), dma((2, depth)), dma((2,)),
             dma((PLANE, 2)), dma((PLANE, 2)), dma, dma,

time: 44.3 us -> 44.1 us (level)
  no operation moved by 1% of the time
where the time goes in v7:
time: 44.1 us; the launch traced here: 43.9 us
  Pallas kernels  43.1 us (98%)
  local copies, waits for them, and re-layouts  0.8 us (2%)
    pallas_call x1, Pallas kernels, body(): pl.pallas_call(functools.partial(kernel, rows, cols, tile_rows, tile_cols...  43.1 us

profile of v7, /device:TPU:0, one launch (start us, length us, event | category | flops | bytes accessed | tf_op | source)
XLA Modules:
  0.0 43.9 jit_solution(699508723551319662)
XLA Ops:
  0.0 43.1 %shard_map.82 = bf16[4,16,4096]{2,1,0:T(8,128)(2,1)S(1)} custom-call(bf16[256,1024]{1,0:T(8,128)(2,1)} %bitcast.5, f32[3,1024]{1,0:T(4,128)} %ratio_hbm.1, bf16[3,64,1024]{2,1,0:T(8,128)(2,1)} %w_hbm.1, f32[16,8,32]{2,1,0:T(8,128)} %ret_hbm.1, f32[1,1024]{1,0:T(1,128)} %bitcast.8, f32[1,1024]{1,0:T(1,128)} %bitcast.9, f32[1,4096]{1,0:T(1,128)} %bitcast.6, ...), custom_call_target="tpu_custom_call" | custom-call | tf_op jit(solution)/shard_map/pallas_call | solution.py:578
  43.1 0.8 %copy.10 = bf16[4,16,4096]{2,1,0:T(8,128)(2,1)} copy(bf16[4,16,4096]{2,1,0:T(8,128)(2,1)S(1)} %shard_map.82) | data formatting | bytes 1048576
